TPU v7x, 128 devices: a whole 4x4x4 slice. The times are simulated.
128 devices in a mesh: space: 8 (over z, core), scene: 16 (over x, y).
Axes of the slice: x: 4, y: 4, z: 4, core: 2. Of those that a mesh axis runs over, the one named last changes fastest.
Arguments:
- pixels: bfloat16 [32, 128, 64, 384], P('scene', 'space'), may hold values from -6 to 6
- dw_kernel: bfloat16 [7, 7, 384], replicated, may hold values from -0.875 to 0.875
- dw_bias: float32 [384], replicated, may hold values from -3 to 3
- norm_gain: float32 [384], replicated, may hold values from 0.25 to 1.75
- w_expand: bfloat16 [384, 1536], replicated, may hold values from -0.3125 to 0.3125
- w_reduce: bfloat16 [1536, 384], replicated, may hold values from -0.15625 to 0.15625
- layer_scale: float32 [384], replicated, may hold values from 0.3 to 1
- pixel_slot: int32 [32, 128, 64], P('scene', 'space'), may hold values from 0 to 255
- intersection: int32 [128, 256], P(('space', 'scene')), may hold values from 0 to 8191, as said below
- parcel_pos: int32 [8192], replicated, may hold values from 0 to 8191, as said below
- parcel_embed: bfloat16 [8192, 384], P(('space', 'scene')), may hold values from -6 to 6
- attn_gain: float32 [384], replicated, may hold values from 0.25 to 1.75
- w_qkv: bfloat16 [384, 1152], replicated, may hold values from -0.91855865 to 0.91855865
- w_out: bfloat16 [384, 384], replicated, may hold values from -0.3125 to 0.3125
- w_class: bfloat16 [384, 20], replicated, may hold values from -10.7165176 to 10.7165176
- labels: int32 [8192], P(('space', 'scene')), may hold values from 0 to 19
Outputs:
- features: bfloat16 [32, 128, 64, 384], P('scene', 'space')
- parcel_state: bfloat16 [8192, 384], P(('space', 'scene'))
- loss: float32 [8192], P(('space', 'scene'))
Inputs may be any that keep to these rules, and one draw needn't show every extreme that they name: `intersection`: row t lists 256 distinct parcels; each owner (positions o * 64 to o * 64 + 63) holds 1 to 3 of them, and in every tile some owner holds exactly 3. `parcel_pos`: each position occurs once.
All inputs are finite; a program needn't handle non-finite values.
Results may differ from a plain program's by a relative error of at most 0.035.
The roundings to bfloat16 on the way count: a program that leaves them out, or rounds other values in their place, can miss the bound.
Values may be sent and summed in bfloat16 or wider, within the bound.
A program may use at most 128 MiB of HBM per device.

v0:
```python
import jax
import jax.numpy as jnp
from jax import lax
from jax.sharding import PartitionSpec as P

CAP = 3
PAR_DEV = 64
HEADS = 6
HEAD_DIM = 64


epsilon = 1e-06


def with_halo(x, sides, width):
    for axis, dim in sides:
        count, length = (lax.axis_size(axis), x.shape[dim])
        up = [(i, (i + 1) % count) for i in range(count - 1)]
        down = [(j, i) for i, j in up]
        last = lax.slice_in_dim(x, length - width, length, axis=dim)
        initial = lax.slice_in_dim(x, 0, width, axis=dim)
        before = lax.ppermute(last, axis, up)
        after = lax.ppermute(initial, axis, down)
        x = jnp.concatenate([before, x, after], axis=dim)
    return x


def layer_norm(values):
    average = jnp.mean(values, axis=-1, keepdims=True)
    centered = values - average
    return centered * lax.rsqrt(jnp.mean(centered * centered, axis=-1, keepdims=True) + epsilon)


def convnext_block(padded, center, dw_kernel, dw_bias, norm_gain, w_expand, w_reduce, layer_scale):
    height = center.shape[1]
    breadth = center.shape[2]
    kernel_f32 = dw_kernel.astype(jnp.float32)
    spatial = jnp.zeros(center.shape, jnp.float32)
    for row_off in range(dw_kernel.shape[0]):
        for col_off in range(dw_kernel.shape[1]):
            window = padded[:, row_off : row_off + height, col_off : col_off + breadth, :]
            spatial = spatial + window.astype(jnp.float32) * kernel_f32[row_off, col_off]
    spatial = spatial + dw_bias
    normed = (layer_norm(spatial) * norm_gain).astype(jnp.bfloat16)
    channels = center.shape[-1]
    flattened = normed.reshape(-1, channels)
    hidden = jax.nn.gelu(
        jnp.dot(flattened, w_expand, preferred_element_type=jnp.float32), approximate=False
    ).astype(jnp.bfloat16)
    branch = jnp.dot(hidden, w_reduce, preferred_element_type=jnp.float32).reshape(center.shape)
    return (center.astype(jnp.float32) + layer_scale * branch).astype(jnp.bfloat16)


def local(
    pixels,
    dw_kernel,
    dw_bias,
    norm_gain,
    w_expand,
    w_reduce,
    layer_scale,
    pixel_slot,
    intersection,
    parcel_pos,
    parcel_embed,
    attn_gain,
    w_qkv,
    w_out,
    w_class,
    labels,
):
    channels = pixels.shape[-1]
    highest = lax.Precision.HIGHEST
    extended = with_halo(pixels, (("space", 1),), 3)
    padded = jnp.pad(extended, ((0, 0), (0, 0), (3, 3), (0, 0)))
    features = convnext_block(
        padded, pixels, dw_kernel, dw_bias, norm_gain, w_expand, w_reduce, layer_scale
    )
    slot_total = intersection.shape[1]
    owners = lax.axis_size("space") * lax.axis_size("scene")
    slot_range = jnp.arange(slot_total, dtype=jnp.int32)
    membership = (slot_range[:, None] == pixel_slot.reshape(-1)[None, :]).astype(jnp.bfloat16)
    slot_sums = jnp.dot(
        membership, features.reshape(-1, channels), preferred_element_type=jnp.float32
    )
    slot_counts = jnp.sum(membership, axis=1, dtype=jnp.float32)
    positions = jnp.take(parcel_pos, intersection[0])
    owner_dev = positions // PAR_DEV
    local_row = (positions % PAR_DEV).astype(jnp.float32)
    earlier = (owner_dev[:, None] == owner_dev[None, :]) & (
        slot_range[None, :] < slot_range[:, None]
    )
    slot_rank = jnp.sum(earlier.astype(jnp.int32), axis=1)
    buffer_slot = owner_dev * CAP + slot_rank
    placer = (jnp.arange(owners * CAP, dtype=jnp.int32)[:, None] == buffer_slot[None, :]).astype(
        jnp.float32
    )
    sent_sums = jnp.dot(placer, slot_sums, precision=highest)
    sent_counts = jnp.dot(placer, slot_counts, precision=highest)
    sent_rows = jnp.dot(placer, local_row, precision=highest)
    arrived = (
        lax.all_to_all(
            sent_sums.reshape(owners, CAP, channels),
            ("space", "scene"),
            split_axis=0,
            concat_axis=0,
            tiled=True,
        ),
        lax.all_to_all(
            sent_counts.reshape(owners, CAP),
            ("space", "scene"),
            split_axis=0,
            concat_axis=0,
            tiled=True,
        ),
        lax.all_to_all(
            sent_rows.reshape(owners, CAP),
            ("space", "scene"),
            split_axis=0,
            concat_axis=0,
            tiled=True,
        ),
    )
    recv_sums = arrived[0].reshape(-1, channels)
    recv_counts = arrived[1].reshape(-1)
    recv_rows = arrived[2].reshape(-1)
    gather_table = (jnp.arange(PAR_DEV, dtype=jnp.float32)[:, None] == recv_rows[None, :]).astype(
        jnp.float32
    )
    parcel_sums = jnp.dot(gather_table, recv_sums, precision=highest)
    parcel_counts = jnp.dot(gather_table, recv_counts, precision=highest)
    tokens = parcel_sums / jnp.maximum(parcel_counts, 1.0)[:, None] + parcel_embed.astype(
        jnp.float32
    )
    attn_in = (layer_norm(tokens) * attn_gain).astype(jnp.bfloat16)
    queries = (
        jnp.dot(attn_in, w_qkv[:, :channels], preferred_element_type=jnp.float32)
        * HEAD_DIM ** (-0.5)
    ).astype(jnp.bfloat16)
    queries = queries.reshape(-1, HEADS, HEAD_DIM)
    w_pair = w_qkv[:, channels:]
    parcels_here = tokens.shape[0]
    key_value = jnp.dot(attn_in, w_pair, preferred_element_type=jnp.float32).astype(jnp.bfloat16)
    top_score = jnp.full((HEADS, parcels_here), -1e30, jnp.float32)
    key_heads = lax.all_gather(
        key_value[:, :channels], ("space", "scene"), axis=0, tiled=True
    ).reshape(-1, HEADS, HEAD_DIM)
    value_heads = lax.all_gather(
        key_value[:, channels:], ("space", "scene"), axis=0, tiled=True
    ).reshape(-1, HEADS, HEAD_DIM)
    scores = jnp.einsum("qhd,khd->hqk", queries, key_heads, preferred_element_type=jnp.float32)
    new_top = jnp.maximum(top_score, jnp.max(scores, axis=-1))
    weights = jnp.exp(scores - new_top[:, :, None])
    row_total = jnp.sum(weights, axis=-1)
    update = jnp.einsum(
        "hqk,khd->qhd",
        weights.astype(jnp.bfloat16),
        value_heads,
        preferred_element_type=jnp.float32,
    )
    weighted = update
    folded = (new_top, row_total, weighted)
    row_total = folded[1]
    weighted = folded[2]
    attended = (
        (weighted / jnp.transpose(row_total)[:, :, None])
        .reshape(parcels_here, channels)
        .astype(jnp.bfloat16)
    )
    parcel_out = tokens + jnp.dot(attended, w_out, preferred_element_type=jnp.float32)
    class_in = layer_norm(parcel_out).astype(jnp.bfloat16)
    logits = jnp.dot(class_in, w_class, preferred_element_type=jnp.float32)
    top_logit = jnp.max(logits, axis=-1, keepdims=True)
    log_total = top_logit[:, 0] + jnp.log(jnp.sum(jnp.exp(logits - top_logit), axis=-1))
    picked = jnp.sum(
        jnp.where(
            jnp.arange(logits.shape[1], dtype=jnp.int32)[None, :] == labels[:, None], logits, 0.0
        ),
        axis=-1,
    )
    return (features, parcel_out.astype(jnp.bfloat16), log_total - picked)


def solution(mesh):
    in_specs = (
        P("scene", "space", None, None),
        P(),
        P(),
        P(),
        P(),
        P(),
        P(),
        P("scene", "space", None),
        P(("space", "scene"), None),
        P(),
        P(("space", "scene"), None),
        P(),
        P(),
        P(),
        P(),
        P(("space", "scene")),
    )
    out_specs = (
        P("scene", "space", None, None),
        P(("space", "scene"), None),
        P(("space", "scene")),
    )
    return jax.shard_map(local, mesh=mesh, in_specs=in_specs, out_specs=out_specs, check_vma=False)
```

profile of v0, /device:TPU:1, one launch (start us, length us, event | category | flops | bytes accessed | tf_op | source)
XLA Modules:
  0.0 303.3 jit_solution(5688462011921432681)
XLA Ops:
  7.2 2.1 fusion.122
  9.3 4.9 %collective-permute-start = (bf16[2,3,64,384]{3,2,1,0:T(8,128)(2,1)}, bf16[2,3,64,384]{3,2,1,0:T(8,128)(2,1)S(1)}, u32[]{:S(2)}, u32[]{:S(2)}) collective-permute-start(bf16[2,3,64,384]{3,2,1,0:T(8,128)(2,1)} %get-tuple-element.58), channel_id=1, source_target_pairs={{0,16},{16,32},{32,48},{48,64},{64,80},{80,96},{96,112},{1,17},{17... | collective-permute-start | bytes 884744 | tf_op jit(solution)/shard_map/ppermute | solution.py:22
  14.2 1.9 collective-permute-start.1
  16.2 0.7 compare_select_fusion
  16.8 2.0 gather_fusion
  18.8 0.7 and_select_fusion.1
  19.5 0.7 and_select_fusion.3
  20.7 0.6 copy-done.6
  21.3 0.9 fusion.73
  22.2 0.8 copy.32
  23.0 10.2 %all-to-all-start = ((f32[128,1,3]{2,1,0:T(1,128)}), f32[128,1,3]{2,1,0:T(1,128)S(1)}, u32[]{:S(2)}, u32[]{:S(2)}) async-start(f32[128,1,3]{2,1,0:T(1,128)} %bitcast.12), calls=%async_computation | async-start | bytes 131072 | tf_op jit(solution)/shard_map/all_to_all | solution.py:116
  33.2 0.8 convert_element_type.208
  34.4 1.2 fusion.71
  35.6 0.7 copy.33
  36.6 0.7 constant_dynamic-update-slice_fusion
  37.3 1.2 fusion.51
  38.6 23.7 %fusion.120 = (f32[2,16,64]{2,1,0:T(8,128)S(1)}, f32[2,16,64,384]{3,2,1,0:T(8,128)S(1)}) fusion(f32[384]{0:T(512)S(1)} %copy-done.11, f32[384]{0:T(512)S(1)} %get-tuple-element.4, bf16[2,22,70,384]{3,2,1,0:T(8,128)(2,1)S(1)} %fusion.51, f32[384]{0:T(512)S(1)} %get-tuple-element.5, f32[384]{0:T(512)S(1)} %get-tuple-element.6, f32[384]{0:T(512)S(1)} %get-tuple-element.7, ...), kind=kLoop, calls=%fused_computation.224 | loop fusion | flops 116389888 | bytes 80301056 | tf_op jit(solution)/shard_map/reduce_sum | solution.py:29
  62.3 0.7 multiply_reduce_fusion
  63.0 1.6 multiply_convert_fusion
  64.6 32.0 %fusion.15 = f32[2048,384]{1,0:T(8,128)} fusion(bf16[1536,384]{1,0:T(8,128)(2,1)S(1)} %copy-done, bf16[2048,384]{1,0:T(8,128)(2,1)} %bitcast.52, bf16[384,1536]{1,0:T(8,128)(2,1)} %param.20), kind=kOutput, calls=%fused_computation.27 | convolution fusion | flops 5036310528 | bytes 7077888 | tf_op jit(solution)/shard_map/dot_general | solution.py:50
  96.7 2.4 fusion.45
  99.1 1.1 copy-done.3
  100.3 0.7 fusion.53
  101.0 9.7 %all-to-all-start.2 = ((f32[128,1,3]{2,1,0:T(1,128)}), f32[128,1,3]{2,1,0:T(1,128)S(1)}, u32[]{:S(2)}, u32[]{:S(2)}) async-start(f32[128,1,3]{2,1,0:T(1,128)} %bitcast.16), calls=%async_computation.2 | async-start | bytes 131072 | tf_op jit(solution)/shard_map/all_to_all | solution.py:109
  110.8 1.3 fusion.68
  112.0 1.1 reshape.238
  113.2 7.1 %all-to-all-done.2 = f32[128,1,3]{2,1,0:T(1,128)S(1)} async-done(((f32[128,1,3]{2,1,0:T(1,128)}), f32[128,1,3]{2,1,0:T(1,128)S(1)}, u32[]{:S(2)}, u32[]{:S(2)}) %all-to-all-start.2) | async-done | bytes 1568 | tf_op jit(solution)/shard_map/all_to_all | solution.py:109
  120.3 4.5 %all-to-all-start.1 = ((f32[128,3,384]{2,1,0:T(4,128)}), f32[128,3,384]{2,1,0:T(4,128)S(1)}, u32[]{:S(2)}, u32[]{:S(2)}) async-start(f32[128,3,384]{2,1,0:T(4,128)} %reshape.238), calls=%async_computation.1 | async-start | bytes 1572864 | tf_op jit(solution)/shard_map/all_to_all | solution.py:102
  124.9 0.5 broadcast.297
  125.4 0.8 reduce.105
  126.4 0.8 reduce.104
  127.5 13.3 %all-to-all-done.1 = f32[128,3,384]{2,1,0:T(4,128)S(1)} async-done(((f32[128,3,384]{2,1,0:T(4,128)}), f32[128,3,384]{2,1,0:T(4,128)S(1)}, u32[]{:S(2)}, u32[]{:S(2)}) %all-to-all-start.1) | async-done | bytes 589856 | tf_op jit(solution)/shard_map/all_to_all | solution.py:102
  141.1 0.5 fusion.124
  141.8 1.0 convolution_convert_fusion
  142.8 0.6 fusion.123
  143.5 0.7 all-gather.3.cloned.1.call-update
  144.2 0.9 fusion.64
  145.3 63.2 %all-gather.5.cloned.1.call-done = bf16[8192,384]{1,0:T(8,128)(2,1)} async-done(((bf16[64,384]{1,0:T(8,128)(2,1)}), bf16[8192,384]{1,0:T(8,128)(2,1)}) %all-gather.5.cloned.1.call-update) | async-done | bytes 6291472 | tf_op jit(solution)/shard_map/all_gather | solution.py:145
  208.4 8.6 %copy.29 = bf16[8192,384]{0,1:T(8,128)(2,1)} copy(bf16[8192,384]{1,0:T(8,128)(2,1)} %all-gather.5.cloned.1.call-done) | data formatting | bytes 12582912 | tf_op jit(solution)/shard_map/all_gather | solution.py:145
  217.0 4.7 %fusion.125 = (f32[6,64]{1,0:T(8,128)S(1)}, f32[6,64,8192]{2,1,0:T(8,128)S(1)}) fusion(bf16[8192,6,64]{0,2,1:T(8,128)(2,1)} %bitcast.48, bf16[64,6,64]{2,1,0:T(8,128)(2,1)S(1)} %reshape.242), kind=kOutput, calls=%fused_computation.228 | convolution fusion | flops 405798528 | bytes 18925056 | tf_op jit(solution)/shard_map/qhd,khd->hqk/dot_general | solution.py:151
  221.7 4.6 %copy-done.1 = f32[6,64,8192]{2,1,0:T(8,128)} copy-done((f32[6,64,8192]{2,1,0:T(8,128)}, f32[6,64,8192]{2,1,0:T(8,128)S(1)}, u32[]{:S(2)}) %copy-start.1) | copy-done | bytes 12582936
  226.3 2.0 fusion.10
  228.3 49.1 %all-gather.3.cloned.1.call-done = bf16[8192,384]{1,0:T(8,128)(2,1)} async-done(((bf16[64,384]{1,0:T(8,128)(2,1)}), bf16[8192,384]{1,0:T(8,128)(2,1)}) %all-gather.3.cloned.1.call-update) | async-done | bytes 6291472 | tf_op jit(solution)/shard_map/all_gather | solution.py:148
  277.3 8.6 %copy.28 = bf16[8192,384]{0,1:T(8,128)(2,1)} copy(bf16[8192,384]{1,0:T(8,128)(2,1)} %all-gather.3.cloned.1.call-done) | data formatting | bytes 12582912 | tf_op jit(solution)/shard_map/all_gather | solution.py:148
  286.0 8.6 %fusion.61 = bf16[64,6,64]{0,2,1:T(8,128)(2,1)S(1)} fusion(bf16[8192,6,64]{0,2,1:T(8,128)(2,1)} %bitcast.49, f32[6,64,8192]{2,1,0:T(8,128)} %copy-done.1, f32[6,64]{1,0:T(8,128)S(1)} %broadcast_maximum_fusion, f32[64,6]{0,1:T(8,128)S(1)} %bitcast.54), kind=kOutput, calls=%fused_computation.77 | convolution fusion | flops 408993792 | bytes 18926592 | tf_op jit(solution)/shard_map/hqk,khd->qhd/dot_general | solution.py:155
  294.6 0.3 fusion.126
  294.9 0.7 multiply_reduce_fusion.1
  295.9 0.5 add_subtract_fusion
  (60 shorter events, 2.8 us)
Async XLA Ops:
  7.2 57.5 %copy-start = (bf16[1536,384]{1,0:T(8,128)(2,1)S(1)}, bf16[1536,384]{1,0:T(8,128)(2,1)}, u32[]{:S(2)}) copy-start(bf16[1536,384]{1,0:T(8,128)(2,1)} %param.21) | copy-start | bytes 3538948
  7.2 29.4 %copy-start.2 = (bf16[2,16,64,384]{3,2,1,0:T(8,128)(2,1)S(1)}, bf16[2,16,64,384]{3,2,1,0:T(8,128)(2,1)}, u32[]{:S(2)}) copy-start(bf16[2,16,64,384]{3,2,1,0:T(8,128)(2,1)} %param.16) | copy-start | bytes 4718596
  7.2 26.8 %copy-start.9 = (s32[2,16,64]{2,1,0:T(8,128)S(1)}, s32[2,16,64]{2,1,0:T(8,128)}, u32[]{:S(2)}) copy-start(s32[2,16,64]{2,1,0:T(8,128)} %param.23) | copy-start | bytes 24580
  9.3 27.3 %collective-permute-start = (bf16[2,3,64,384]{3,2,1,0:T(8,128)(2,1)}, bf16[2,3,64,384]{3,2,1,0:T(8,128)(2,1)S(1)}, u32[]{:S(2)}, u32[]{:S(2)}) collective-permute-start(bf16[2,3,64,384]{3,2,1,0:T(8,128)(2,1)} %get-tuple-element.58), channel_id=1, source_target_pairs={{0,16},{16,32},{32,48},{48,64},{64,80},{80,96},{96,112},{1,17},{17... | collective-permute-start | bytes 884744 | tf_op jit(solution)/shard_map/ppermute | solution.py:22
  14.2 23.1 %collective-permute-start.1 = (bf16[2,3,64,384]{3,2,1,0:T(8,128)(2,1)}, bf16[2,3,64,384]{3,2,1,0:T(8,128)(2,1)S(1)}, u32[]{:S(2)}, u32[]{:S(2)}) collective-permute-start(bf16[2,3,64,384]{3,2,1,0:T(8,128)(2,1)} %get-tuple-element.59), channel_id=1, source_target_pairs={{16,0},{32,16},{48,32},{64,48},{80,64},{96,80},{112,96},{17,1},{33... | collective-permute-start | bytes 884744 | tf_op jit(solution)/shard_map/ppermute | solution.py:23
  20.4 2.6 copy-start.10
  20.7 0.7 copy-start.6
  23.0 78.0 %all-to-all-start = ((f32[128,1,3]{2,1,0:T(1,128)}), f32[128,1,3]{2,1,0:T(1,128)S(1)}, u32[]{:S(2)}, u32[]{:S(2)}) async-start(f32[128,1,3]{2,1,0:T(1,128)} %bitcast.12), calls=%async_computation | async-start | bytes 131072 | tf_op jit(solution)/shard_map/all_to_all | solution.py:116
  37.3 1.3 copy-start.11
  62.3 0.7 copy-start.12
  64.6 32.1 %copy-start.13 = (f32[384]{0:T(512)S(1)}, f32[384]{0:T(512)}, u32[]{:S(2)}) copy-start(f32[384]{0:T(512)} %param.22) | copy-start | bytes 4612
  99.1 1.1 copy-start.3
  101.0 40.2 %copy-start.7 = (bf16[64,384]{1,0:T(8,128)(2,1)S(1)}, bf16[64,384]{1,0:T(8,128)(2,1)}, u32[]{:S(2)}) copy-start(bf16[64,384]{1,0:T(8,128)(2,1)} %param.26) | copy-start | bytes 147460
  101.0 19.3 %all-to-all-start.2 = ((f32[128,1,3]{2,1,0:T(1,128)}), f32[128,1,3]{2,1,0:T(1,128)S(1)}, u32[]{:S(2)}, u32[]{:S(2)}) async-start(f32[128,1,3]{2,1,0:T(1,128)} %bitcast.16), calls=%async_computation.2 | async-start | bytes 131072 | tf_op jit(solution)/shard_map/all_to_all | solution.py:109
  110.7 31.1 %copy-start.4 = (bf16[384,1152]{1,0:T(8,128)(2,1)S(1)}, bf16[384,1152]{1,0:T(8,128)(2,1)}, u32[]{:S(2)}) copy-start(bf16[384,1152]{1,0:T(8,128)(2,1)} %param.28) | copy-start | bytes 2654212
  120.3 20.5 %all-to-all-start.1 = ((f32[128,3,384]{2,1,0:T(4,128)}), f32[128,3,384]{2,1,0:T(4,128)S(1)}, u32[]{:S(2)}, u32[]{:S(2)}) async-start(f32[128,3,384]{2,1,0:T(4,128)} %reshape.238), calls=%async_computation.1 | async-start | bytes 1572864 | tf_op jit(solution)/shard_map/all_to_all | solution.py:102
  124.8 83.6 %all-gather.5.cloned.1.call-start = ((), (), s32[]{:S(2)}) async-start(), calls=%async_computation.4 | async-start | bytes 6340608 | tf_op jit(solution)/shard_map/all_gather | solution.py:145
  143.5 133.9 %all-gather.3.cloned.1.call-start = ((), (), s32[]{:S(2)}) async-start(), calls=%async_computation.3 | async-start | bytes 6340608 | tf_op jit(solution)/shard_map/all_gather | solution.py:148
  221.7 4.6 %copy-start.1 = (f32[6,64,8192]{2,1,0:T(8,128)}, f32[6,64,8192]{2,1,0:T(8,128)S(1)}, u32[]{:S(2)}) copy-start(f32[6,64,8192]{2,1,0:T(8,128)S(1)} %get-tuple-element.67) | copy-start | bytes 37748740
  286.0 8.6 %copy-start.5 = (bf16[384,384]{1,0:T(8,128)(2,1)S(1)}, bf16[384,384]{1,0:T(8,128)(2,1)}, u32[]{:S(2)}) copy-start(bf16[384,384]{1,0:T(8,128)(2,1)} %param.29) | copy-start | bytes 884740
  286.0 9.7 %copy-start.8 = (bf16[384,20]{0,1:T(8,128)(2,1)S(1)}, bf16[384,20]{0,1:T(8,128)(2,1)}, u32[]{:S(2)}) copy-start(bf16[384,20]{0,1:T(8,128)(2,1)} %param.30) | copy-start | bytes 46084
  286.0 9.9 %copy-start.14 = (s32[64]{0:T(128)S(1)}, s32[64]{0:T(128)}, u32[]{:S(2)}) copy-start(s32[64]{0:T(128)} %param.31) | copy-start | bytes 772
Sparse Core Ops, SparseCore 0:
  143.6 64.8 all-gather.4
  211.5 65.8 all-gather.2
where the time goes:
time: 304 us; the launch traced here: 303 us
  waiting for transfers between devices  133 us (44%)
  matrix products  52.4 us (17%)
  other arithmetic  38.2 us (13%)
  local copies, waits for them, and re-layouts  33.4 us (11%)
  starting transfers between devices  31.4 us (10%)
  between operations  14.5 us (5%)
    all_gather x1, waiting for transfers between devices, local(): lax.all_gather(key_value[:, :channels], ('space', 'scene'), axis=0, tiled...  63.2 us
    all_gather x1, waiting for transfers between devices, local(): lax.all_gather(key_value[:, channels:], ('space', 'scene'), axis=0, tiled...  49.1 us
    dot_general x1, matrix products, convnext_block(): jnp.dot(hidden, w_reduce, preferred_element_type=jnp.float32)  32 us
    reduce_sum x1, other arithmetic, layer_norm(): average = jnp.mean(values, axis=-1, keepdims=True)  23.7 us
    all_to_all x1, waiting for transfers between devices, local(): lax.all_to_all(sent_sums.reshape(owners, CAP, channels), ('space', 'scene...  13.3 us
    all_to_all x1, starting transfers between devices, local(): lax.all_to_all(sent_rows.reshape(owners, CAP), ('space', 'scene'), split_...  10.2 us
    all_to_all x1, starting transfers between devices, local(): lax.all_to_all(sent_counts.reshape(owners, CAP), ('space', 'scene'), spli...  9.74 us
    all_gather x1, local copies, waits for them, and re-layouts, local(): lax.all_gather(key_value[:, channels:], ('space', 'scene'), axis=0, tiled...  8.63 us
  transfers between devices with their start and end apart: 7, of which 4 were waited for; matrix products, arithmetic and copies ran while one was open for 31% of the time, Pallas kernels for 0%

commit v1 on v0

v1 whole, which is shorter than its diff:
```python
import jax
import jax.numpy as jnp
from jax import lax
from jax.experimental import pallas as pl
from jax.experimental.pallas import tpu as pltpu
from jax.sharding import PartitionSpec as P

EPS = 1e-06
N_SPACE = 8
N_SCENE = 16
DEVS = N_SPACE * N_SCENE
PAR = 64
CAP = 3
MSG = 16
F32 = jnp.float32
BF16 = jnp.bfloat16
MESH = pl.DeviceIdType.MESH


def mm(a, b):
    return jnp.dot(a, b, preferred_element_type=F32)


def mm_t(a, b):
    return lax.dot_general(a, b, (((0,), (0,)), ((), ())), preferred_element_type=F32)


def mm_nt(a, b):
    return lax.dot_general(a, b, (((1,), (1,)), ((), ())), preferred_element_type=F32)


def onehot(cond):
    return jnp.where(cond, 1.0, 0.0).astype(BF16)


def iota(shape, dim):
    return lax.broadcasted_iota(jnp.int32, shape, dim)


def layer_norm(x):
    centered = x - jnp.mean(x, axis=-1, keepdims=True)
    return centered * lax.rsqrt(jnp.mean(centered * centered, axis=-1, keepdims=True) + EPS)


def gelu(x):
    return 0.5 * x * (1.0 + lax.erf(x * 0.7071067811865476))


def block_kernel(pix_hbm, up_ref, dn_ref, k_ref, bias_ref, gain_ref, w1_ref, w2_ref, ls_ref, slot_ref, pos_ref,
                 feat_ref, send_ref, xs, kb, vs, sp, ssum, scnt, shm, stg, sem):
    i = pl.program_id(0)

    @pl.when(i == 0)
    def _():
        cps = [pltpu.make_async_copy(pix_hbm.at[s], xs.at[s, pl.ds(3, 16)], sem.at[s]) for s in range(2)]
        for cp in cps:
            cp.start()
        for s in range(2):
            xs[s, 0:3] = up_ref[s]
            xs[s, 19:22] = dn_ref[s]
        for a in range(7):
            k32 = k_ref[a].astype(F32)
            for b in range(7):
                kb[a * 7 + b] = jnp.broadcast_to(k32[b:b + 1, :], (16, 384)).astype(BF16)
        j = iota((64, 448), 1)
        shm[...] = onehot(j % 64 == iota((64, 448), 0) + j // 64 - 3)
        ssum[...] = jnp.zeros_like(ssum)
        scnt[...] = jnp.zeros_like(scnt)
        for cp in cps:
            cp.wait()

    s = i // 4
    r0 = (i % 4) * 4
    for r in range(4):
        for c in range(3):
            cs = pl.ds(c * 128, 128)
            acc = [None] * 7
            for a in range(7):
                x = xs[s, r0 + r + a, :, :, cs]
                for b in range(7):
                    p = x * kb[a * 7 + b, :, cs][None]
                    acc[b] = p if acc[b] is None else acc[b] + p
            for b in range(7):
                vs[b, :, :, cs] = acc[b]
        sp[pl.ds(r * 64, 64), :] = mm(shm[...], vs[...].reshape(448, 384)) + bias_ref[...][None, :]
    nrm = (layer_norm(sp[...]) * gain_ref[...][None, :]).astype(BF16)
    out = None
    for h in range(6):
        hs = pl.ds(h * 256, 256)
        d = mm(gelu(mm(nrm, w1_ref[:, hs])).astype(BF16), w2_ref[hs, :])
        out = d if out is None else out + d
    cen = xs[s, pl.ds(r0 + 3, 4)].reshape(256, 384)
    f = (cen.astype(F32) + ls_ref[...][None, :] * out).astype(BF16)
    feat_ref[...] = f.reshape(feat_ref.shape)
    m = onehot(iota((256, 256), 0) == slot_ref[...].reshape(1, 256))
    ssum[...] += mm(m, f)
    scnt[...] += mm(m, jnp.ones((256, 128), BF16))

    @pl.when(i == pl.num_programs(0) - 1)
    def _():
        pos = pos_ref[...]
        lane = iota((256, 128), 1)
        mine = pos // PAR == lane
        rank = mm(onehot(iota((256, 256), 1) < iota((256, 256), 0)), onehot(mine))
        cnt = scnt[...]
        high = jnp.floor(cnt * (1.0 / 64.0))
        meta = jnp.where(lane == 64, high, jnp.where(lane == 65, cnt - 64.0 * high, jnp.where(lane == pos % PAR, 1.0, 0.0)))
        body = jnp.concatenate([ssum[...], meta], axis=1).astype(BF16)
        for j in range(CAP):
            placed = mm_t(onehot(mine & (rank == j)), body)
            for c in range(4):
                stg[pl.ds(4 * j + c, 128, stride=MSG), :] = placed[:, c * 128:(c + 1) * 128]
        for q in range(4 * CAP, MSG):
            stg[pl.ds(q, 128, stride=MSG), :] = jnp.zeros((128, 128), F32)
        send_ref[...] = stg[...].reshape(128, MSG, 128).astype(BF16)


def block(pixels, up, dn, dw_kernel, bias, gain, w1, w2, ls, slot, pos):
    full = lambda a: pl.BlockSpec(a.shape, lambda i, n=a.ndim: (0,) * n)
    args = (
        pixels.reshape(2, 16, 4, 16, 384), up.reshape(2, 3, 4, 16, 384), dn.reshape(2, 3, 4, 16, 384),
        dw_kernel, bias, gain, w1, w2, ls, slot.reshape(8, 1, 256), pos.reshape(256, 1),
    )
    specs = [pl.BlockSpec(memory_space=pl.ANY)] + [full(a) for a in args[1:9]]
    specs += [pl.BlockSpec((1, 1, 256), lambda i: (i, 0, 0)), full(args[10])]
    feat, send = pl.pallas_call(
        block_kernel,
        grid=(8,),
        out_shape=(jax.ShapeDtypeStruct((2, 16, 4, 16, 384), BF16), jax.ShapeDtypeStruct((128, MSG, 128), BF16)),
        in_specs=specs,
        out_specs=(
            pl.BlockSpec((1, 4, 4, 16, 384), lambda i: (i // 4, i % 4, 0, 0, 0)),
            pl.BlockSpec((128, MSG, 128), lambda i: (0, 0, 0)),
        ),
        scratch_shapes=[
            pltpu.VMEM((2, 22, 4, 16, 384), BF16),
            pltpu.VMEM((49, 16, 384), BF16),
            pltpu.VMEM((7, 4, 16, 384), BF16),
            pltpu.VMEM((256, 384), F32),
            pltpu.VMEM((256, 384), F32),
            pltpu.VMEM((256, 128), F32),
            pltpu.VMEM((64, 448), BF16),
            pltpu.VMEM((2048, 128), F32),
            pltpu.SemaphoreType.DMA((2,)),
        ],
        compiler_params=pltpu.CompilerParams(vmem_limit_bytes=40 << 20),
        name="block",
    )(*args)
    return feat.reshape(2, 16, 64, 384), send


def parcel_kernel(send, embed_ref, gain_ref, wqkv_ref, wout_ref, wcls_ref, lab_ref, state_ref, loss_ref,
                  recv, x32, ain, aq, ak, qb, kb, vb, outb, inb, ssem, rsem):
    sp = lax.axis_index("space")
    sc = lax.axis_index("scene")
    me = sp * N_SCENE + sc

    barrier = pltpu.get_barrier_semaphore()

    def greet(k, carry):
        o = lax.rem(me + k, DEVS)
        pl.semaphore_signal(barrier, inc=1, device_id=(o // N_SCENE, o % N_SCENE), device_id_type=MESH)
        return carry

    lax.fori_loop(1, DEVS, greet, 0)
    pl.semaphore_wait(barrier, DEVS - 1)

    def push(src, dst, n, dev):
        return pltpu.make_async_remote_copy(
            src_ref=src, dst_ref=dst, send_sem=ssem.at[n], recv_sem=rsem.at[n], device_id=dev, device_id_type=MESH
        )

    here = (sp, sc)

    def scatter(k, carry):
        o = lax.rem(me + k, DEVS)
        push(send.at[o], recv.at[me], 0, (o // N_SCENE, o % N_SCENE)).start()
        return carry

    lax.fori_loop(1, DEVS, scatter, 0)
    recv[me] = send[me]
    push(send.at[pl.ds(0, DEVS - 1)], recv.at[pl.ds(0, DEVS - 1)], 0, here).wait()

    x32[...] = recv[...].reshape(DEVS * MSG, 128).astype(F32)
    row = lambda q: x32[pl.ds(q, DEVS, stride=MSG), :].astype(BF16)
    picks = jnp.concatenate([row(4 * j + 3) for j in range(CAP)], axis=0)
    body = jnp.concatenate(
        [jnp.concatenate([row(4 * j + c) for c in range(4)], axis=1) for j in range(CAP)], axis=0
    )
    pooled = mm_t(picks, body)[:PAR]
    lane = iota((PAR, 128), 1)
    tail = pooled[:, 384:]
    count = jnp.sum(jnp.where(lane == 64, 64.0 * tail, jnp.where(lane == 65, tail, 0.0)), axis=-1, keepdims=True)
    tokens = pooled[:, :384] / jnp.maximum(count, 1.0) + embed_ref[...].astype(F32)
    attn_in = (layer_norm(tokens) * gain_ref[...][None, :]).astype(BF16)
    ain[...] = attn_in
    aq[sp] = attn_in
    ak[sc] = attn_in

    def send_q(k, carry):
        push(ain, aq.at[sp], 1, (lax.rem(sp + k, N_SPACE), sc)).start()
        return carry

    def send_k(k, carry):
        push(ain, ak.at[sc], 2, (sp, lax.rem(sc + k, N_SCENE))).start()
        return carry

    lax.fori_loop(1, N_SPACE, send_q, 0)
    lax.fori_loop(1, N_SCENE, send_k, 0)
    push(aq.at[pl.ds(0, N_SPACE - 1)], aq.at[pl.ds(0, N_SPACE - 1)], 1, here).wait()
    qb[...] = (mm(aq[...].reshape(N_SPACE * PAR, 384), wqkv_ref[:, :384]) * 0.125).astype(BF16)
    push(ak.at[pl.ds(0, N_SCENE - 1)], ak.at[pl.ds(0, N_SCENE - 1)], 2, here).wait()
    keys_in = ak[...].reshape(N_SCENE * PAR, 384)
    kb[...] = mm(keys_in, wqkv_ref[:, 384:768]).astype(BF16)
    values = mm(keys_in, wqkv_ref[:, 768:]).astype(BF16)
    for p in range(3):
        vb[:, p * 256:p * 256 + 128] = values[:, p * 128:(p + 1) * 128]
        vb[:, p * 256 + 128:(p + 1) * 256] = jnp.ones((N_SCENE * PAR, 128), BF16)

    rows = N_SPACE * PAR // 2
    lanes = iota((rows, 128), 1)
    for t in range(2):
        ts = pl.ds(t * rows, rows)
        stats = jnp.zeros((rows, 128), F32)
        for p in range(3):
            ps = pl.ds(p * 128, 128)
            q = qb[ts, ps]
            mixed = None
            for u in range(2):
                h = 2 * p + u
                scores = mm_nt(jnp.where((lanes >= 64) == (u == 1), q, jnp.zeros_like(q)), kb[:, ps])
                top = jnp.max(scores, axis=-1, keepdims=True)
                weights = jnp.exp(scores - top).astype(BF16)
                both = mm(weights, vb[:, p * 256:(p + 1) * 256])
                total = both[:, 128:]
                part = both[:, :128] / total
                mixed = part if u == 0 else jnp.where(lanes < 64, mixed, part)
                lse = top + jnp.log(total)
                s0 = lse.astype(BF16).astype(F32)
                s1 = (lse - s0).astype(BF16).astype(F32)
                s2 = lse - s0 - s1
                stats = jnp.where(lanes == h, s0, jnp.where(lanes == 8 + h, s1, jnp.where(lanes == 16 + h, s2, stats)))
            outb[pl.ds(t * 4, 4), :, ps] = mixed.astype(BF16).reshape(4, PAR, 128)
        outb[pl.ds(t * 4, 4), :, 384:] = stats.astype(BF16).reshape(4, PAR, 128)

    def send_o(k, carry):
        o = lax.rem(sp + k, N_SPACE)
        push(outb.at[o], inb.at[sp], 3, (o, sc)).start()
        return carry

    lax.fori_loop(1, N_SPACE, send_o, 0)
    inb[sp] = outb[sp]
    push(outb.at[pl.ds(0, N_SPACE - 1)], inb.at[pl.ds(0, N_SPACE - 1)], 3, here).wait()

    spread = onehot((iota((128, 384), 0) % 8 == iota((128, 384), 1) // 64) & (iota((128, 384), 0) < 24))
    lse = mm(inb[:, :, 384:].reshape(N_SPACE * PAR, 128), spread).reshape(N_SPACE, PAR, 384)
    share = jnp.exp(lse - jnp.max(lse, axis=0, keepdims=True))
    attended = jnp.sum(share * inb[:, :, :384].astype(F32), axis=0) / jnp.sum(share, axis=0)
    state = tokens + mm(attended.astype(BF16), wout_ref[...])
    state_ref[...] = state.astype(BF16)
    class_in = layer_norm(state).astype(BF16)
    logits = lax.dot_general(wcls_ref[...], class_in, (((0,), (1,)), ((), ())), preferred_element_type=F32)
    peak = jnp.max(logits, axis=0, keepdims=True)
    log_total = peak + jnp.log(jnp.sum(jnp.exp(logits - peak), axis=0, keepdims=True))
    picked = jnp.sum(jnp.where(iota(logits.shape, 0) == lab_ref[...], logits, 0.0), axis=0, keepdims=True)
    loss_ref[...] = log_total - picked


def parcels(send, embed, gain, wqkv, wout, wcls, labels):
    vmem = pl.BlockSpec(memory_space=pltpu.VMEM)
    state, loss = pl.pallas_call(
        parcel_kernel,
        out_shape=(jax.ShapeDtypeStruct((PAR, 384), BF16), jax.ShapeDtypeStruct((1, PAR), F32)),
        in_specs=[vmem] * 7,
        out_specs=(vmem, vmem),
        scratch_shapes=[
            pltpu.VMEM((DEVS, MSG, 128), BF16),
            pltpu.VMEM((DEVS * MSG, 128), F32),
            pltpu.VMEM((PAR, 384), BF16),
            pltpu.VMEM((N_SPACE, PAR, 384), BF16),
            pltpu.VMEM((N_SCENE, PAR, 384), BF16),
            pltpu.VMEM((N_SPACE * PAR, 384), BF16),
            pltpu.VMEM((N_SCENE * PAR, 384), BF16),
            pltpu.VMEM((N_SCENE * PAR, 768), BF16),
            pltpu.VMEM((N_SPACE, PAR, 512), BF16),
            pltpu.VMEM((N_SPACE, PAR, 512), BF16),
            pltpu.SemaphoreType.DMA((4,)),
            pltpu.SemaphoreType.DMA((4,)),
        ],
        compiler_params=pltpu.CompilerParams(vmem_limit_bytes=40 << 20, collective_id=0, has_side_effects=True),
        name="parcels",
    )(send, embed, gain, wqkv, wout, wcls, labels.reshape(1, PAR))
    return state, loss.reshape(PAR)


def local(pixels, dw_kernel, dw_bias, norm_gain, w_expand, w_reduce, layer_scale, pixel_slot, intersection,
          parcel_pos, parcel_embed, attn_gain, w_qkv, w_out, w_class, labels):
    count = lax.axis_size("space")
    ahead = [(i, i + 1) for i in range(count - 1)]
    up = lax.ppermute(pixels[:, 13:], "space", ahead)
    dn = lax.ppermute(pixels[:, :3], "space", [(j, i) for i, j in ahead])
    positions = jnp.take(parcel_pos, intersection[0])
    features, send = block(
        pixels, up, dn, dw_kernel, dw_bias, norm_gain, w_expand, w_reduce, layer_scale, pixel_slot, positions
    )
    state, loss = parcels(send, parcel_embed, attn_gain, w_qkv, w_out, w_class, labels)
    return features, state, loss


def solution(mesh):
    in_specs = (
        P("scene", "space", None, None), P(), P(), P(), P(), P(), P(), P("scene", "space", None),
        P(("space", "scene"), None), P(), P(("space", "scene"), None), P(), P(), P(), P(), P(("space", "scene")),
    )
    out_specs = (P("scene", "space", None, None), P(("space", "scene"), None), P(("space", "scene")))
    return jax.shard_map(local, mesh=mesh, in_specs=in_specs, out_specs=out_specs, check_vma=False)
```

time: 304 us -> 99.1 us (0.33)
  waiting for transfers between devices: 133 us -> 0.01 us
  Pallas kernels: 0 us -> 79.4 us
  matrix products: 52.4 us -> 0 us
  other arithmetic: 38.2 us -> 2.01 us
  starting transfers between devices: 31.4 us -> 6.84 us
  local copies, waits for them, and re-layouts: 33.4 us -> 9.45 us
  between operations: 14.5 us -> 0.89 us
    all_gather x2 -> x0, waiting for transfers between devices: 112 us -> none  [the longest x1 63.2 us: local(): lax.all_gather(key_value[:, :channels], ('space', 'scene'), axis=0, tiled...]
    pallas_call x0 -> x2, Pallas kernels: none -> 79.4 us  [the longest x1 46 us: parcels(): pl.pallas_call(parcel_kernel, out_shape=(jax.ShapeDtypeStruct((PAR, 384),...]
    dot_general x13 -> x0, matrix products: 52.4 us -> none  [the longest x1 32 us: convnext_block(): jnp.dot(hidden, w_reduce, preferred_element_type=jnp.float32)]
    reduce_sum x8 -> x0, other arithmetic: 27.8 us -> none  [the longest x1 23.7 us: layer_norm(): average = jnp.mean(values, axis=-1, keepdims=True)]
    all_to_all x3 -> x0, starting transfers between devices: 24.4 us -> none  [the longest x1 10.2 us: local(): lax.all_to_all(sent_rows.reshape(owners, CAP), ('space', 'scene'), split_...]
    all_to_all x3 -> x0, waiting for transfers between devices: 20.4 us -> none  [the longest x1 13.3 us: local(): lax.all_to_all(sent_sums.reshape(owners, CAP, channels), ('space', 'scene...]
    all_gather x2 -> x0, local copies, waits for them, and re-layouts: 17.2 us -> none  [the longest x1 8.63 us: local(): lax.all_gather(key_value[:, channels:], ('space', 'scene'), axis=0, tiled...]
    convert_element_type x3 -> x0, other arithmetic: 4.81 us -> none  [the longest x1 2.41 us: convnext_block(): (center.astype(jnp.float32) + layer_scale * branch).astype(jnp.bfloat16)]
  transfers between devices with their start and end apart: 7 -> 2, of which waited for: 4 -> 0; matrix products, arithmetic and copies ran while one was open for 31% -> 7% of each run, Pallas kernels for 0% -> 0%
where the time goes in v1:
time: 99.1 us; the launch traced here: 98.6 us
  Pallas kernels  79.4 us (80%)
  local copies, waits for them, and re-layouts  9.45 us (10%)
  starting transfers between devices  6.84 us (7%)
  other arithmetic  2.01 us (2%)
    pallas_call x1, Pallas kernels, parcels(): pl.pallas_call(parcel_kernel, out_shape=(jax.ShapeDtypeStruct((PAR, 384),...  46 us
    pallas_call x1, Pallas kernels, block(): pl.pallas_call(block_kernel, grid=(8,), out_shape=(jax.ShapeDtypeStruct((...  33.5 us
    ppermute x1, starting transfers between devices, local(): up = lax.ppermute(pixels[:, 13:], 'space', ahead)  4.92 us
    unnamed x31, local copies, waits for them, and re-layouts  3.32 us
    gather x2, local copies, waits for them, and re-layouts, local(): positions = jnp.take(parcel_pos, intersection[0])  2.51 us
    slice x1, local copies, waits for them, and re-layouts, local(): dn = lax.ppermute(pixels[:, :3], 'space', [(j, i) for i, j in ahead])  2.08 us
    select_n x2, other arithmetic, local(): positions = jnp.take(parcel_pos, intersection[0])  2.01 us
  transfers between devices with their start and end apart: 2, of which 0 were waited for; matrix products, arithmetic and copies ran while one was open for 7% of the time, Pallas kernels for 0%

profile of v1, /device:TPU:1, one launch (start us, length us, event | category | flops | bytes accessed | tf_op | source)
XLA Modules:
  0.0 98.6 jit_solution(3475738331631477114)
XLA Ops:
  0.6 0.0 copy-start
  0.6 0.0 copy-start.1
  0.7 0.0 copy-start.13
  0.7 0.0 copy-start.7
  0.7 0.0 copy-start.8
  0.7 0.0 copy-start.9
  0.7 0.0 copy-start.2
  0.7 0.0 copy-start.10
  0.7 2.1 %fusion.1 = (bf16[2,3,64,384]{3,2,1,0:T(8,128)(2,1)}, bf16[2,3,64,384]{3,2,1,0:T(8,128)(2,1)}) fusion(bf16[2,16,64,384]{3,2,1,0:T(8,128)(2,1)} %param.16), kind=kLoop, calls=%fused_computation.5 | loop fusion | bytes 1179648 | tf_op jit(solution)/shard_map/slice | solution.py:301
  2.8 4.9 %collective-permute-start = (bf16[2,3,64,384]{3,2,1,0:T(8,128)(2,1)}, bf16[2,3,64,384]{3,2,1,0:T(8,128)(2,1)S(1)}, u32[]{:S(2)}, u32[]{:S(2)}) collective-permute-start(bf16[2,3,64,384]{3,2,1,0:T(8,128)(2,1)} %get-tuple-element.12), channel_id=1, source_target_pairs={{0,16},{16,32},{32,48},{48,64},{64,80},{80,96},{96,112},{1,17},{17... | collective-permute-start | bytes 884744 | tf_op jit(solution)/shard_map/ppermute | solution.py:300
  7.7 1.9 %collective-permute-start.1 = (bf16[2,3,64,384]{3,2,1,0:T(8,128)(2,1)}, bf16[2,3,64,384]{3,2,1,0:T(8,128)(2,1)S(1)}, u32[]{:S(2)}, u32[]{:S(2)}) collective-permute-start(bf16[2,3,64,384]{3,2,1,0:T(8,128)(2,1)} %get-tuple-element.11), channel_id=1, source_target_pairs={{16,0},{32,16},{48,32},{64,48},{80,64},{96,80},{112,96},{17,1},{33... | collective-permute-start | bytes 884744 | tf_op jit(solution)/shard_map/ppermute | solution.py:301
  9.7 1.5 %copy.20 = s32[256,1]{1,0:T(8,128)} copy(s32[256,1]{0,1:T(1,128)} %bitcast.14) | data formatting | bytes 2048 | tf_op jit(solution)/shard_map/squeeze | solution.py:302
  11.1 1.0 %fusion = s32[256]{0:T(256)S(1)} fusion(s32[256,1]{1,0:T(8,128)} %copy.20), kind=kLoop, calls=%fused_computation.3 | loop fusion | flops 768 | bytes 2048 | tf_op jit(solution)/shard_map/jit(_take)/jit(_where)/select_n | solution.py:302
  12.1 0.0 copy-done
  12.2 1.7 %gather_fusion = s32[256]{0:T(256)S(1)} fusion(s32[8192]{0:T(1024)S(1)} %copy-done, s32[1024]{0:T(1024)S(1)} %pad_clamp_fusion), kind=kCustom, calls=%fused_computation | custom fusion | bytes 3072 | tf_op jit(solution)/shard_map/jit(_take)/gather | solution.py:302
  13.9 0.8 copy.23
  14.7 0.0 copy-done.13
  14.7 0.1 reshape.91.slot_ref
  14.8 0.9 copy.24.wcls_ref
  15.6 1.0 %and_select_fusion.pos_ref = s32[256,1]{1,0:T(8,128)S(1)} fusion(s32[256,1]{1,0:T(8,128)} %copy.23, s32[256,1]{1,0:T(8,128)} %copy.20), kind=kLoop, calls=%fused_computation.2 | loop fusion | flops 1792 | bytes 3072 | tf_op jit(solution)/shard_map/jit(_take)/select_n | solution.py:302
  16.6 0.0 collective-permute-done
  16.6 0.0 collective-permute-done.1
  16.6 0.0 copy-done.1
  16.7 0.0 copy-done.7
  16.7 0.0 copy-done.8
  16.7 0.0 copy-done.9
  16.7 0.0 copy-done.2
  16.7 0.0 copy-done.10
  16.7 0.0 copy-start.3
  16.7 1.3 %copy-done.3 = bf16[1536,384]{1,0:T(8,128)(2,1)S(1)} copy-done((bf16[1536,384]{1,0:T(8,128)(2,1)S(1)}, bf16[1536,384]{1,0:T(8,128)(2,1)}, u32[]{:S(2)}) %copy-start.3) | copy-done | bytes 1179672
  18.0 0.0 copy-start.4
  18.0 0.0 copy-start.5
  18.0 0.0 copy-start.6
  18.0 0.0 copy-start.11
  18.0 0.0 copy-start.12
  18.0 33.5 %block.1 = (bf16[2,16,4,16,384]{4,3,2,1,0:T(8,128)(2,1)}, bf16[128,16,128]{2,1,0:T(8,128)(2,1)S(1)}) custom-call(bf16[2,16,4,16,384]{4,3,2,1,0:T(8,128)(2,1)S(1)} %bitcast.8, bf16[2,3,4,16,384]{4,3,2,1,0:T(8,128)(2,1)S(1)} %bitcast.9, bf16[2,3,4,16,384]{4,3,2,1,0:T(8,128)(2,1)S(1)} %bitcast.10, bf16[7,7,384]{2,1,0:T(8,128)(2,1)S(1)} %copy-done.7, ...), custom_call_target="tpu_custom_call" | custom-call | tf_op jit(solution)/shard_map/block/pallas_call | solution.py:126
  51.5 0.0 copy-done.4
  51.5 0.0 copy-done.5
  51.5 0.0 copy-done.6
  51.5 0.0 copy-done.11
  51.5 0.0 copy-done.12
  51.5 46.0 %parcels.1 = (bf16[64,384]{1,0:T(8,128)(2,1)S(1)}, f32[1,64]{1,0:T(1,128)S(1)}) custom-call(bf16[128,16,128]{2,1,0:T(8,128)(2,1)S(1)} %get-tuple-element.8.send, bf16[64,384]{1,0:T(8,128)(2,1)S(1)} %copy-done.6, f32[384]{0:T(512)S(1)} %copy-done.11, bf16[384,1152]{1,0:T(8,128)(2,1)S(1)} %copy-done.4, bf16[384,384]{1,0:T(8,128)(2,1)S(1)} %copy-done.5, ...), custom_call_target="tpu_custom_call" | custom-call | tf_op jit(solution)/shard_map/parcels/pallas_call | solution.py:271
  97.5 0.6 copy.27
  98.1 0.5 copy.28
  (1 shorter events, 0.0 us)
Async XLA Ops:
  0.6 11.5 %copy-start = (s32[8192]{0:T(1024)S(1)}, s32[8192]{0:T(1024)}, u32[]{:S(2)}) copy-start(s32[8192]{0:T(1024)} %param.25) | copy-start | bytes 98308
  0.6 16.0 %copy-start.1 = (bf16[2,16,64,384]{3,2,1,0:T(8,128)(2,1)S(1)}, bf16[2,16,64,384]{3,2,1,0:T(8,128)(2,1)}, u32[]{:S(2)}) copy-start(bf16[2,16,64,384]{3,2,1,0:T(8,128)(2,1)} %param.16) | copy-start | bytes 4718596
  0.7 14.0 %copy-start.13 = (s32[2,16,64]{2,1,0:T(8,128)S(1)}, s32[2,16,64]{2,1,0:T(8,128)}, u32[]{:S(2)}) copy-start(s32[2,16,64]{2,1,0:T(8,128)} %param.23) | copy-start | bytes 24580
  0.7 16.0 %copy-start.7 = (bf16[7,7,384]{2,1,0:T(8,128)(2,1)S(1)}, bf16[7,7,384]{2,1,0:T(8,128)(2,1)}, u32[]{:S(2)}) copy-start(bf16[7,7,384]{2,1,0:T(8,128)(2,1)} %k_ref.1) | copy-start | bytes 112900
  0.7 16.0 %copy-start.8 = (f32[384]{0:T(512)S(1)}, f32[384]{0:T(512)}, u32[]{:S(2)}) copy-start(f32[384]{0:T(512)} %bias_ref.1) | copy-start | bytes 4612
  0.7 16.0 %copy-start.9 = (f32[384]{0:T(512)S(1)}, f32[384]{0:T(512)}, u32[]{:S(2)}) copy-start(f32[384]{0:T(512)} %gain_ref.2) | copy-start | bytes 4612
  0.7 16.0 %copy-start.2 = (bf16[384,1536]{1,0:T(8,128)(2,1)S(1)}, bf16[384,1536]{1,0:T(8,128)(2,1)}, u32[]{:S(2)}) copy-start(bf16[384,1536]{1,0:T(8,128)(2,1)} %w1_ref.1) | copy-start | bytes 3538948
  0.7 16.0 %copy-start.10 = (f32[384]{0:T(512)S(1)}, f32[384]{0:T(512)}, u32[]{:S(2)}) copy-start(f32[384]{0:T(512)} %ls_ref.1) | copy-start | bytes 4612
  2.8 13.8 %collective-permute-start = (bf16[2,3,64,384]{3,2,1,0:T(8,128)(2,1)}, bf16[2,3,64,384]{3,2,1,0:T(8,128)(2,1)S(1)}, u32[]{:S(2)}, u32[]{:S(2)}) collective-permute-start(bf16[2,3,64,384]{3,2,1,0:T(8,128)(2,1)} %get-tuple-element.12), channel_id=1, source_target_pairs={{0,16},{16,32},{32,48},{48,64},{64,80},{80,96},{96,112},{1,17},{17... | collective-permute-start | bytes 884744 | tf_op jit(solution)/shard_map/ppermute | solution.py:300
  7.7 8.9 %collective-permute-start.1 = (bf16[2,3,64,384]{3,2,1,0:T(8,128)(2,1)}, bf16[2,3,64,384]{3,2,1,0:T(8,128)(2,1)S(1)}, u32[]{:S(2)}, u32[]{:S(2)}) collective-permute-start(bf16[2,3,64,384]{3,2,1,0:T(8,128)(2,1)} %get-tuple-element.11), channel_id=1, source_target_pairs={{16,0},{32,16},{48,32},{64,48},{80,64},{96,80},{112,96},{17,1},{33... | collective-permute-start | bytes 884744 | tf_op jit(solution)/shard_map/ppermute | solution.py:301
  16.7 1.3 %copy-start.3 = (bf16[1536,384]{1,0:T(8,128)(2,1)S(1)}, bf16[1536,384]{1,0:T(8,128)(2,1)}, u32[]{:S(2)}) copy-start(bf16[1536,384]{1,0:T(8,128)(2,1)} %w2_ref.1) | copy-start | bytes 3538948
  18.0 33.5 %copy-start.4 = (bf16[384,1152]{1,0:T(8,128)(2,1)S(1)}, bf16[384,1152]{1,0:T(8,128)(2,1)}, u32[]{:S(2)}) copy-start(bf16[384,1152]{1,0:T(8,128)(2,1)} %wqkv_ref.1) | copy-start | bytes 2654212
  18.0 33.5 %copy-start.5 = (bf16[384,384]{1,0:T(8,128)(2,1)S(1)}, bf16[384,384]{1,0:T(8,128)(2,1)}, u32[]{:S(2)}) copy-start(bf16[384,384]{1,0:T(8,128)(2,1)} %wout_ref.1) | copy-start | bytes 884740
  18.0 33.5 %copy-start.6 = (bf16[64,384]{1,0:T(8,128)(2,1)S(1)}, bf16[64,384]{1,0:T(8,128)(2,1)}, u32[]{:S(2)}) copy-start(bf16[64,384]{1,0:T(8,128)(2,1)} %embed_ref.1) | copy-start | bytes 147460
  18.0 33.5 %copy-start.11 = (f32[384]{0:T(512)S(1)}, f32[384]{0:T(512)}, u32[]{:S(2)}) copy-start(f32[384]{0:T(512)} %gain_ref.3) | copy-start | bytes 4612
  18.0 33.5 %copy-start.12 = (s32[64]{0:T(128)S(1)}, s32[64]{0:T(128)}, u32[]{:S(2)}) copy-start(s32[64]{0:T(128)} %param.31) | copy-start | bytes 772

commit v2 on v1

v2 whole, which is shorter than its diff:
```python
import jax
import jax.numpy as jnp
from jax import lax
from jax.experimental import pallas as pl
from jax.experimental.pallas import tpu as pltpu
from jax.sharding import PartitionSpec as P

EPS = 1e-06
N_SPACE = 8
N_SCENE = 16
DEVS = N_SPACE * N_SCENE
PAR = 64
CAP = 3
MSG = 16
F32 = jnp.float32
BF16 = jnp.bfloat16
MESH = pl.DeviceIdType.MESH


def mm(a, b):
    return jnp.dot(a, b, preferred_element_type=F32)


def mm_t(a, b):
    return lax.dot_general(a, b, (((0,), (0,)), ((), ())), preferred_element_type=F32)


def mm_nt(a, b):
    return lax.dot_general(a, b, (((1,), (1,)), ((), ())), preferred_element_type=F32)


def onehot(cond):
    return jnp.where(cond, 1.0, 0.0).astype(BF16)


def iota(shape, dim):
    return lax.broadcasted_iota(jnp.int32, shape, dim)


def layer_norm(x):
    centered = x - jnp.mean(x, axis=-1, keepdims=True)
    return centered * lax.rsqrt(jnp.mean(centered * centered, axis=-1, keepdims=True) + EPS)


def gelu(x):
    return 0.5 * x * (1.0 + lax.erf(x * 0.7071067811865476))


def fused_kernel(pix_hbm, w1_hbm, w2_hbm, wqkv_hbm, wout_hbm, embed_hbm, k_ref, bias_ref, gain_ref, ls_ref, slot_ref,
                 inter_ref, ppos_ref, again_ref, wcls_ref, lab_ref, feat_hbm, state_ref, loss_ref,
                 xs, taps, vs, sp32, nb, fb, ssum, scnt, shm, w1, w2, wqkv, wout, embed, send, recv, x32, ain, aq, ak,
                 qb, kb, vb, outb, inb, lsem, fsem, ssem, rsem):
    sp = lax.axis_index("space")
    sc = lax.axis_index("scene")
    me = sp * N_SCENE + sc
    here = (sp, sc)

    loads = [pltpu.make_async_copy(pix_hbm.at[s], xs.at[s, pl.ds(3, 16)], lsem.at[s]) for s in range(2)]
    pairs = ((w1_hbm, w1), (w2_hbm, w2), (wqkv_hbm, wqkv), (wout_hbm, wout), (embed_hbm, embed))
    loads += [pltpu.make_async_copy(a, b, lsem.at[2 + n]) for n, (a, b) in enumerate(pairs)]
    for cp in loads:
        cp.start()

    barrier = pltpu.get_barrier_semaphore()

    def greet(k, carry):
        o = lax.rem(me + k, DEVS)
        pl.semaphore_signal(barrier, inc=1, device_id=(o // N_SCENE, o % N_SCENE), device_id_type=MESH)
        return carry

    lax.fori_loop(1, DEVS, greet, 0)

    def push(src, dst, n, dev):
        return pltpu.make_async_remote_copy(
            src_ref=src, dst_ref=dst, send_sem=ssem.at[n], recv_sem=rsem.at[n], device_id=dev, device_id_type=MESH
        )

    to_prev = push(xs.at[:, pl.ds(3, 3)], xs.at[:, pl.ds(19, 3)], 4, (lax.rem(sp + N_SPACE - 1, N_SPACE), sc))
    to_next = push(xs.at[:, pl.ds(16, 3)], xs.at[:, pl.ds(0, 3)], 5, (lax.rem(sp + 1, N_SPACE), sc))
    first, last = sp == 0, sp == N_SPACE - 1

    @pl.when(first)
    def _():
        xs[:, 0:3] = jnp.zeros((2, 3, 4, 16, 384), BF16)

    @pl.when(last)
    def _():
        xs[:, 19:22] = jnp.zeros((2, 3, 4, 16, 384), BF16)

    for a in range(7):
        k32 = k_ref[a].astype(F32)
        for b in range(7):
            taps[a * 7 + b] = jnp.broadcast_to(k32[b:b + 1, :], (16, 384)).astype(BF16)
    j = iota((64, 448), 1)
    shm[...] = onehot(j % 64 == iota((64, 448), 0) + j // 64 - 3)
    ssum[...] = jnp.zeros_like(ssum)
    scnt[...] = jnp.zeros_like(scnt)

    def place(k):
        inner = k < 4
        s = lax.rem(k, 4) // 2
        r0 = jnp.where(inner, 4 + 4 * lax.rem(k, 2), 12 * lax.rem(k, 2))
        return s, r0

    def conv(k):
        s, r0 = place(k)
        slot = lax.rem(k, 2)

        def piece(r, c):
            cs = pl.ds(c * 128, 128)
            acc = [None] * 7
            for a in range(7):
                x = xs[s, r0 + r + a, :, :, cs]
                for b in range(7):
                    p = x * taps[a * 7 + b, :, cs][None]
                    acc[b] = p if acc[b] is None else acc[b] + p
            for b in range(7):
                vs[r, b, :, :, cs] = acc[b]

        def row(r):
            sp32[pl.ds(r * 64, 64), :] = mm(shm[...], vs[r].reshape(448, 384)) + bias_ref[...][None, :]

        def norm():
            nb[slot] = (layer_norm(sp32[...]) * gain_ref[...][None, :]).astype(BF16)

        steps = []
        for r in range(4):
            steps += [lambda r=r, c=c: piece(r, c) for c in range(3)]
            steps.append(lambda r=r: row(r))
        return steps + [norm]

    def mlp(k):
        s, r0 = place(k)
        box = {}

        def part(h):
            hs = pl.ds(h * 256, 256)
            d = mm(gelu(mm(nb[lax.rem(k, 2)], w1[:, hs])).astype(BF16), w2[hs, :])
            box["out"] = d if h == 0 else box["out"] + d

        def finish():
            cen = xs[s, pl.ds(r0 + 3, 4)].reshape(256, 384)
            f = (cen.astype(F32) + ls_ref[...][None, :] * box["out"]).astype(BF16)
            fb[k] = f.reshape(4, 4, 16, 384)
            save(k).start()
            slots = jnp.concatenate([slot_ref[s, pl.ds(r0 + r, 1), :] for r in range(4)], axis=1)
            m = onehot(iota((256, 256), 0) == slots)
            ssum[...] += mm(m, f)
            scnt[...] += mm(m, jnp.ones((256, 128), BF16))

        return [lambda h=h: part(h) for h in range(6)] + [finish]

    def save(k):
        s, r0 = place(k)
        return pltpu.make_async_copy(fb.at[k], feat_hbm.at[s, pl.ds(r0, 4)], fsem.at[k])

    def run(*lists):
        total = max(len(x) for x in lists)
        done = [0] * len(lists)
        for t in range(total):
            for n, x in enumerate(lists):
                while done[n] < len(x) and done[n] * total < (t + 1) * len(x):
                    x[done[n]]()
                    done[n] += 1

    loads[0].wait()
    loads[1].wait()
    run(conv(0))
    loads[2].wait()
    loads[3].wait()

    def stage(k, carry):
        @pl.when(k == 1)
        def _():
            pl.semaphore_wait(barrier, DEVS - 1)

            @pl.when(jnp.logical_not(first))
            def _():
                to_prev.start()

            @pl.when(jnp.logical_not(last))
            def _():
                to_next.start()

        @pl.when(k == 3)
        def _():
            @pl.when(jnp.logical_not(first))
            def _():
                to_prev.wait_send()
                to_next.wait_recv()

            @pl.when(jnp.logical_not(last))
            def _():
                to_next.wait_send()
                to_prev.wait_recv()

        run(mlp(k), conv(k + 1))
        return carry

    lax.fori_loop(0, 7, stage, 0)
    run(mlp(7))

    inter = inter_ref[...]
    hot = onehot(iota((64, 256), 0) == inter // 128)
    low = iota((128, 256), 0) == inter % 128
    table = ppos_ref[...]
    pick = lambda t: jnp.sum(jnp.where(low, mm_t(t.astype(F32).astype(BF16), hot), 0.0), axis=0, keepdims=True)
    owner = pick(table // PAR)
    inrow = pick(table % PAR)
    sub = iota((128, 256), 0).astype(F32)
    mine = sub == owner
    at_row = onehot(sub == inrow)
    rank = mm(onehot(mine), onehot(iota((256, 256), 0) < iota((256, 256), 1)))
    lane = iota((256, 128), 1)
    high = jnp.floor(scnt[...] * (1.0 / 64.0))
    counts = jnp.where(lane == 64, high, jnp.where(lane == 65, scnt[...] - 64.0 * high, 0.0)).astype(BF16)
    sums = ssum[...].astype(BF16)
    for j in range(CAP):
        sel = onehot(mine & (rank == j))
        placed = mm(sel, sums)
        for c in range(3):
            x32[pl.ds(4 * j + c, DEVS, stride=MSG), :] = placed[:, c * 128:(c + 1) * 128]
        x32[pl.ds(4 * j + 3, DEVS, stride=MSG), :] = mm_nt(sel, at_row) + mm(sel, counts)
    for q in range(4 * CAP, MSG):
        x32[pl.ds(q, DEVS, stride=MSG), :] = jnp.zeros((DEVS, 128), F32)
    send[...] = x32[...].reshape(DEVS, MSG, 128).astype(BF16)

    def scatter(k, carry):
        o = lax.rem(me + k, DEVS)
        push(send.at[o], recv.at[me], 0, (o // N_SCENE, o % N_SCENE)).start()
        return carry

    lax.fori_loop(1, DEVS, scatter, 0)
    recv[me] = send[me]
    push(send.at[pl.ds(0, DEVS - 1)], recv.at[pl.ds(0, DEVS - 1)], 0, here).wait()

    x32[...] = recv[...].reshape(DEVS * MSG, 128).astype(F32)
    row = lambda q: x32[pl.ds(q, DEVS, stride=MSG), :].astype(BF16)
    picks = jnp.concatenate([row(4 * j + 3) for j in range(CAP)], axis=0)
    body = jnp.concatenate(
        [jnp.concatenate([row(4 * j + c) for c in range(4)], axis=1) for j in range(CAP)], axis=0
    )
    pooled = mm_t(picks, body)[:PAR]
    lane = iota((PAR, 128), 1)
    tail = pooled[:, 384:]
    count = jnp.sum(jnp.where(lane == 64, 64.0 * tail, jnp.where(lane == 65, tail, 0.0)), axis=-1, keepdims=True)
    for cp in loads[4:]:
        cp.wait()
    tokens = pooled[:, :384] / jnp.maximum(count, 1.0) + embed[...].astype(F32)
    attn_in = (layer_norm(tokens) * again_ref[...][None, :]).astype(BF16)
    ain[...] = attn_in
    aq[sp] = attn_in
    ak[sc] = attn_in

    def send_q(k, carry):
        push(ain, aq.at[sp], 1, (lax.rem(sp + k, N_SPACE), sc)).start()
        return carry

    def send_k(k, carry):
        push(ain, ak.at[sc], 2, (sp, lax.rem(sc + k, N_SCENE))).start()
        return carry

    lax.fori_loop(1, N_SPACE, send_q, 0)
    lax.fori_loop(1, N_SCENE, send_k, 0)
    push(aq.at[pl.ds(0, N_SPACE - 1)], aq.at[pl.ds(0, N_SPACE - 1)], 1, here).wait()
    qb[...] = (mm(aq[...].reshape(N_SPACE * PAR, 384), wqkv[:, :384]) * 0.125).astype(BF16)
    push(ak.at[pl.ds(0, N_SCENE - 1)], ak.at[pl.ds(0, N_SCENE - 1)], 2, here).wait()
    keys_in = ak[...].reshape(N_SCENE * PAR, 384)
    kb[...] = mm(keys_in, wqkv[:, 384:768]).astype(BF16)
    values = mm(keys_in, wqkv[:, 768:]).astype(BF16)
    for p in range(3):
        vb[:, p * 256:p * 256 + 128] = values[:, p * 128:(p + 1) * 128]
        vb[:, p * 256 + 128:(p + 1) * 256] = jnp.ones((N_SCENE * PAR, 128), BF16)

    rows = N_SPACE * PAR // 2
    lanes = iota((rows, 128), 1)
    for t in range(2):
        ts = pl.ds(t * rows, rows)
        stats = jnp.zeros((rows, 128), F32)
        for p in range(3):
            ps = pl.ds(p * 128, 128)
            q = qb[ts, ps]
            mixed = None
            for u in range(2):
                h = 2 * p + u
                scores = mm_nt(jnp.where((lanes >= 64) == (u == 1), q, jnp.zeros_like(q)), kb[:, ps])
                top = jnp.max(scores, axis=-1, keepdims=True)
                weights = jnp.exp(scores - top).astype(BF16)
                both = mm(weights, vb[:, p * 256:(p + 1) * 256])
                total = both[:, 128:]
                part = both[:, :128] / total
                mixed = part if u == 0 else jnp.where(lanes < 64, mixed, part)
                lse = top + jnp.log(total)
                s0 = lse.astype(BF16).astype(F32)
                s1 = (lse - s0).astype(BF16).astype(F32)
                s2 = lse - s0 - s1
                stats = jnp.where(lanes == h, s0, jnp.where(lanes == 8 + h, s1, jnp.where(lanes == 16 + h, s2, stats)))
            outb[pl.ds(t * 4, 4), :, ps] = mixed.astype(BF16).reshape(4, PAR, 128)
        outb[pl.ds(t * 4, 4), :, 384:] = stats.astype(BF16).reshape(4, PAR, 128)

    def send_o(k, carry):
        o = lax.rem(sp + k, N_SPACE)
        push(outb.at[o], inb.at[sp], 3, (o, sc)).start()
        return carry

    lax.fori_loop(1, N_SPACE, send_o, 0)
    inb[sp] = outb[sp]
    push(outb.at[pl.ds(0, N_SPACE - 1)], inb.at[pl.ds(0, N_SPACE - 1)], 3, here).wait()

    spread = onehot((iota((128, 384), 0) % 8 == iota((128, 384), 1) // 64) & (iota((128, 384), 0) < 24))
    lse = mm(inb[:, :, 384:].reshape(N_SPACE * PAR, 128), spread).reshape(N_SPACE, PAR, 384)
    share = jnp.exp(lse - jnp.max(lse, axis=0, keepdims=True))
    attended = jnp.sum(share * inb[:, :, :384].astype(F32), axis=0) / jnp.sum(share, axis=0)
    state = tokens + mm(attended.astype(BF16), wout[...])
    state_ref[...] = state.astype(BF16)
    class_in = layer_norm(state).astype(BF16)
    logits = mm_nt(wcls_ref[...], class_in)
    peak = jnp.max(logits, axis=0, keepdims=True)
    log_total = peak + jnp.log(jnp.sum(jnp.exp(logits - peak), axis=0, keepdims=True))
    picked = jnp.sum(jnp.where(iota(logits.shape, 0) == lab_ref[...], logits, 0.0), axis=0, keepdims=True)
    loss_ref[...] = log_total - picked

    def drain(k, carry):
        save(k).wait()
        return carry

    lax.fori_loop(0, 8, drain, 0)


def local(pixels, dw_kernel, dw_bias, norm_gain, w_expand, w_reduce, layer_scale, pixel_slot, intersection,
          parcel_pos, parcel_embed, attn_gain, w_qkv, w_out, w_class, labels):
    vmem = pl.BlockSpec(memory_space=pltpu.VMEM)
    hbm = pl.BlockSpec(memory_space=pl.ANY)
    dma = pltpu.SemaphoreType.DMA
    features, state, loss = pl.pallas_call(
        fused_kernel,
        out_shape=(
            jax.ShapeDtypeStruct((2, 16, 4, 16, 384), BF16),
            jax.ShapeDtypeStruct((PAR, 384), BF16),
            jax.ShapeDtypeStruct((1, PAR), F32),
        ),
        in_specs=[hbm] * 6 + [vmem] * 10,
        out_specs=(hbm, vmem, vmem),
        scratch_shapes=[
            pltpu.VMEM((2, 22, 4, 16, 384), BF16),
            pltpu.VMEM((49, 16, 384), BF16),
            pltpu.VMEM((4, 7, 4, 16, 384), BF16),
            pltpu.VMEM((256, 384), F32),
            pltpu.VMEM((2, 256, 384), BF16),
            pltpu.VMEM((8, 4, 4, 16, 384), BF16),
            pltpu.VMEM((256, 384), F32),
            pltpu.VMEM((256, 128), F32),
            pltpu.VMEM((64, 448), BF16),
            pltpu.VMEM((384, 1536), BF16),
            pltpu.VMEM((1536, 384), BF16),
            pltpu.VMEM((384, 1152), BF16),
            pltpu.VMEM((384, 384), BF16),
            pltpu.VMEM((PAR, 384), BF16),
            pltpu.VMEM((DEVS, MSG, 128), BF16),
            pltpu.VMEM((DEVS, MSG, 128), BF16),
            pltpu.VMEM((DEVS * MSG, 128), F32),
            pltpu.VMEM((PAR, 384), BF16),
            pltpu.VMEM((N_SPACE, PAR, 384), BF16),
            pltpu.VMEM((N_SCENE, PAR, 384), BF16),
            pltpu.VMEM((N_SPACE * PAR, 384), BF16),
            pltpu.VMEM((N_SCENE * PAR, 384), BF16),
            pltpu.VMEM((N_SCENE * PAR, 768), BF16),
            pltpu.VMEM((N_SPACE, PAR, 512), BF16),
            pltpu.VMEM((N_SPACE, PAR, 512), BF16),
            dma((7,)),
            dma((8,)),
            dma((6,)),
            dma((6,)),
        ],
        compiler_params=pltpu.CompilerParams(vmem_limit_bytes=63 << 20, collective_id=0, has_side_effects=True),
        name="fused",
    )(
        pixels.reshape(2, 16, 4, 16, 384), w_expand, w_reduce, w_qkv, w_out, parcel_embed, dw_kernel, dw_bias, norm_gain,
        layer_scale, pixel_slot, intersection, parcel_pos.reshape(64, 128), attn_gain, w_class.T, labels.reshape(1, PAR),
    )
    return features.reshape(2, 16, 64, 384), state, loss.reshape(PAR)


def solution(mesh):
    in_specs = (
        P("scene", "space", None, None), P(), P(), P(), P(), P(), P(), P("scene", "space", None),
        P(("space", "scene"), None), P(), P(("space", "scene"), None), P(), P(), P(), P(), P(("space", "scene")),
    )
    out_specs = (P("scene", "space", None, None), P(("space", "scene"), None), P(("space", "scene")))
    return jax.shard_map(local, mesh=mesh, in_specs=in_specs, out_specs=out_specs, check_vma=False)
```

time: 99.1 us -> 80.1 us (0.81)
  the two profiles are of different devices: /device:TPU:1 before, /device:TPU:25 now
where the time goes in v2:
time: 80.1 us; the launch traced here: 79.9 us
  Pallas kernels  75.4 us (94%)
  local copies, waits for them, and re-layouts  3.86 us (5%)
    pallas_call x1, Pallas kernels, local(): pl.pallas_call(fused_kernel, out_shape=(jax.ShapeDtypeStruct((2, 16, 4, 1...  75.4 us
    unnamed x7, local copies, waits for them, and re-layouts  3.86 us

profile of v2, /device:TPU:25, one launch (start us, length us, event | category | flops | bytes accessed | tf_op | source)
XLA Modules:
  0.0 79.9 jit_solution(12391977988913193108)
XLA Ops:
  0.6 75.4 %fused.1 = (bf16[2,16,4,16,384]{4,3,2,1,0:T(8,128)(2,1)}, bf16[64,384]{1,0:T(8,128)(2,1)}, f32[1,64]{1,0:T(1,128)}) custom-call(bf16[2,16,4,16,384]{4,3,2,1,0:T(8,128)(2,1)} %bitcast.7, bf16[384,1536]{1,0:T(8,128)(2,1)} %w1_hbm.1, bf16[1536,384]{1,0:T(8,128)(2,1)} %w2_hbm.1, bf16[384,1152]{1,0:T(8,128)(2,1)} %wqkv_hbm.1, bf16[384,384]{1,0:T(8,128)(2,1)} %wout_hbm.1, ...), custom_call_target="tpu_custom_call" | custom-call | tf_op jit(solution)/shard_map/fused/pallas_call | solution.py:335
  76.0 0.0 copy-start
  76.0 0.0 copy-start.1
  76.0 2.7 %copy.22 = bf16[2,16,64,384]{3,2,1,0:T(8,128)(2,1)} copy(bf16[2,16,64,384]{3,2,1,0:T(8,128)(2,1)} %bitcast.6) | data formatting | bytes 3145728
  78.8 0.0 copy-done
  78.8 0.6 copy.23
  79.4 0.0 copy-done.1
  79.4 0.5 copy.24
Async XLA Ops:
  76.0 2.7 %copy-start = (bf16[64,384]{1,0:T(8,128)(2,1)S(1)}, bf16[64,384]{1,0:T(8,128)(2,1)}, u32[]{:S(2)}) copy-start(bf16[64,384]{1,0:T(8,128)(2,1)} %get-tuple-element.13) | copy-start | bytes 147460
  76.0 3.4 %copy-start.1 = (f32[1,64]{1,0:T(1,128)S(1)}, f32[1,64]{1,0:T(1,128)}, u32[]{:S(2)}) copy-start(f32[1,64]{1,0:T(1,128)} %get-tuple-element.8) | copy-start | bytes 772

commit v3 on v2

--- a/solution.py
+++ b/solution.py
@@ -15,6 +15,12 @@
 F32 = jnp.float32
 BF16 = jnp.bfloat16
 MESH = pl.DeviceIdType.MESH
+FLAT = pl.DeviceIdType.LOGICAL
+GROUP = 8
+HOPS = (
+    (0, 0), (0, 1), (0, 3), (1, 0), (3, 0), (1, 1), (1, 3), (3, 1),
+    (3, 3), (2, 0), (0, 2), (2, 1), (2, 3), (1, 2), (3, 2), (2, 2),
+)
 
 
 def mm(a, b):
@@ -48,8 +54,8 @@
 
 def fused_kernel(pix_hbm, w1_hbm, w2_hbm, wqkv_hbm, wout_hbm, embed_hbm, k_ref, bias_ref, gain_ref, ls_ref, slot_ref,
                  inter_ref, ppos_ref, again_ref, wcls_ref, lab_ref, feat_hbm, state_ref, loss_ref,
-                 xs, taps, vs, sp32, nb, fb, ssum, scnt, shm, w1, w2, wqkv, wout, embed, send, recv, x32, ain, aq, ak,
-                 qb, kb, vb, outb, inb, lsem, fsem, ssem, rsem):
+                 xs, taps, vs, sp32, nb, hid, fb, ssum, scnt, shm, w1, w2, wqkv, wout, embed, send, recv, x32, ain, aq, ak,
+                 qb, tops, mixes, outb, inb, lsem, fsem, ssem, rsem, all_in):
     sp = lax.axis_index("space")
     sc = lax.axis_index("scene")
     me = sp * N_SCENE + sc
@@ -63,12 +69,10 @@
 
     barrier = pltpu.get_barrier_semaphore()
 
-    def greet(k, carry):
-        o = lax.rem(me + k, DEVS)
-        pl.semaphore_signal(barrier, inc=1, device_id=(o // N_SCENE, o % N_SCENE), device_id_type=MESH)
-        return carry
-
-    lax.fori_loop(1, DEVS, greet, 0)
+    for k in range(1, N_SPACE):
+        pl.semaphore_signal(barrier, inc=1, device_id=(lax.rem(sp + k, N_SPACE), sc), device_id_type=MESH)
+    for k in range(1, N_SCENE):
+        pl.semaphore_signal(barrier, inc=1, device_id=(sp, lax.rem(sc + k, N_SCENE)), device_id_type=MESH)
 
     def push(src, dst, n, dev):
         return pltpu.make_async_remote_copy(
@@ -131,16 +135,14 @@
 
     def mlp(k):
         s, r0 = place(k)
-        box = {}
 
         def part(h):
-            hs = pl.ds(h * 256, 256)
-            d = mm(gelu(mm(nb[lax.rem(k, 2)], w1[:, hs])).astype(BF16), w2[hs, :])
-            box["out"] = d if h == 0 else box["out"] + d
+            hs = pl.ds(h * 512, 512)
+            hid[:, hs] = gelu(mm(nb[lax.rem(k, 2)], w1[:, hs])).astype(BF16)
 
         def finish():
             cen = xs[s, pl.ds(r0 + 3, 4)].reshape(256, 384)
-            f = (cen.astype(F32) + ls_ref[...][None, :] * box["out"]).astype(BF16)
+            f = (cen.astype(F32) + ls_ref[...][None, :] * mm(hid[...], w2[...])).astype(BF16)
             fb[k] = f.reshape(4, 4, 16, 384)
             save(k).start()
             slots = jnp.concatenate([slot_ref[s, pl.ds(r0 + r, 1), :] for r in range(4)], axis=1)
@@ -148,7 +150,7 @@
             ssum[...] += mm(m, f)
             scnt[...] += mm(m, jnp.ones((256, 128), BF16))
 
-        return [lambda h=h: part(h) for h in range(6)] + [finish]
+        return [lambda h=h: part(h) for h in range(3)] + [finish]
 
     def save(k):
         s, r0 = place(k)
@@ -172,7 +174,9 @@
     def stage(k, carry):
         @pl.when(k == 1)
         def _():
-            pl.semaphore_wait(barrier, DEVS - 1)
+            pl.semaphore_wait(barrier, N_SPACE + N_SCENE - 2)
+            for m in range(1, N_SCENE):
+                pl.semaphore_signal(all_in, inc=1, device_id=(sp, lax.rem(sc + m, N_SCENE)), device_id_type=MESH)
 
             @pl.when(jnp.logical_not(first))
             def _():
@@ -225,12 +229,20 @@
         x32[pl.ds(q, DEVS, stride=MSG), :] = jnp.zeros((DEVS, 128), F32)
     send[...] = x32[...].reshape(DEVS, MSG, 128).astype(BF16)
 
-    def scatter(k, carry):
-        o = lax.rem(me + k, DEVS)
-        push(send.at[o], recv.at[me], 0, (o // N_SCENE, o % N_SCENE)).start()
-        return carry
-
-    lax.fori_loop(1, DEVS, scatter, 0)
+    pl.semaphore_wait(all_in, N_SCENE - 1)
+    z, core, x, y = sp // 2, lax.rem(sp, 2), sc // 4, lax.rem(sc, 4)
+    space_at = [(lax.rem(z + d // 2, 4) * 2 + lax.rem(core + d % 2, 2)) * N_SCENE for d in range(N_SPACE)]
+    scene_at = [lax.rem(x + d // 4, 4) * 4 + lax.rem(y + d % 4, 4) for d in range(N_SCENE)]
+    ring = (0, 1, 2, 1)
+    far = sorted(
+        ((-ring[a // 2] - ring[b // 4] - ring[b % 4], a, b) for a in range(N_SPACE) for b in range(N_SCENE) if a + b > 0)
+    )
+    for _, a, b in far:
+        o = space_at[a] + scene_at[b]
+        pltpu.make_async_remote_copy(
+            src_ref=send.at[o], dst_ref=recv.at[me], send_sem=ssem.at[0], recv_sem=rsem.at[0],
+            device_id=o, device_id_type=FLAT,
+        ).start()
     recv[me] = send[me]
     push(send.at[pl.ds(0, DEVS - 1)], recv.at[pl.ds(0, DEVS - 1)], 0, here).wait()
 
@@ -250,60 +262,74 @@
     attn_in = (layer_norm(tokens) * again_ref[...][None, :]).astype(BF16)
     ain[...] = attn_in
     aq[sp] = attn_in
-    ak[sc] = attn_in
+    ak[0] = attn_in
 
     def send_q(k, carry):
         push(ain, aq.at[sp], 1, (lax.rem(sp + k, N_SPACE), sc)).start()
         return carry
 
-    def send_k(k, carry):
-        push(ain, ak.at[sc], 2, (sp, lax.rem(sc + k, N_SCENE))).start()
-        return carry
-
     lax.fori_loop(1, N_SPACE, send_q, 0)
-    lax.fori_loop(1, N_SCENE, send_k, 0)
+    groups = N_SCENE // GROUP
+    for n in range(1, N_SCENE):
+        dx, dy = HOPS[n]
+        to = lax.rem(sc // 4 + dx, 4) * 4 + lax.rem(lax.rem(sc, 4) + dy, 4)
+        push(ain, ak.at[n], 6 + n // GROUP, (sp, to)).start()
     push(aq.at[pl.ds(0, N_SPACE - 1)], aq.at[pl.ds(0, N_SPACE - 1)], 1, here).wait()
     qb[...] = (mm(aq[...].reshape(N_SPACE * PAR, 384), wqkv[:, :384]) * 0.125).astype(BF16)
-    push(ak.at[pl.ds(0, N_SCENE - 1)], ak.at[pl.ds(0, N_SCENE - 1)], 2, here).wait()
-    keys_in = ak[...].reshape(N_SCENE * PAR, 384)
-    kb[...] = mm(keys_in, wqkv[:, 384:768]).astype(BF16)
-    values = mm(keys_in, wqkv[:, 768:]).astype(BF16)
-    for p in range(3):
-        vb[:, p * 256:p * 256 + 128] = values[:, p * 128:(p + 1) * 128]
-        vb[:, p * 256 + 128:(p + 1) * 256] = jnp.ones((N_SCENE * PAR, 128), BF16)
 
     rows = N_SPACE * PAR // 2
     lanes = iota((rows, 128), 1)
-    for t in range(2):
-        ts = pl.ds(t * rows, rows)
-        stats = jnp.zeros((rows, 128), F32)
-        for p in range(3):
-            ps = pl.ds(p * 128, 128)
-            q = qb[ts, ps]
-            mixed = None
-            for u in range(2):
-                h = 2 * p + u
-                scores = mm_nt(jnp.where((lanes >= 64) == (u == 1), q, jnp.zeros_like(q)), kb[:, ps])
-                top = jnp.max(scores, axis=-1, keepdims=True)
-                weights = jnp.exp(scores - top).astype(BF16)
-                both = mm(weights, vb[:, p * 256:(p + 1) * 256])
-                total = both[:, 128:]
-                part = both[:, :128] / total
-                mixed = part if u == 0 else jnp.where(lanes < 64, mixed, part)
-                lse = top + jnp.log(total)
-                s0 = lse.astype(BF16).astype(F32)
-                s1 = (lse - s0).astype(BF16).astype(F32)
-                s2 = lse - s0 - s1
-                stats = jnp.where(lanes == h, s0, jnp.where(lanes == 8 + h, s1, jnp.where(lanes == 16 + h, s2, stats)))
-            outb[pl.ds(t * 4, 4), :, ps] = mixed.astype(BF16).reshape(4, PAR, 128)
-        outb[pl.ds(t * 4, 4), :, 384:] = stats.astype(BF16).reshape(4, PAR, 128)
-
-    def send_o(k, carry):
-        o = lax.rem(sp + k, N_SPACE)
-        push(outb.at[o], inb.at[sp], 3, (o, sc)).start()
-        return carry
-
-    lax.fori_loop(1, N_SPACE, send_o, 0)
+    ones = jnp.ones((GROUP * PAR, 128), BF16)
+    for g in range(groups):
+        low = max(GROUP * g, 1)
+        got = pl.ds(low, GROUP * (g + 1) - low)
+        push(ak.at[got], ak.at[got], 6 + g, here).wait()
+        keys_in = ak[pl.ds(GROUP * g, GROUP)].reshape(GROUP * PAR, 384)
+        keys = mm(keys_in, wqkv[:, 384:768]).astype(BF16)
+        values = mm(keys_in, wqkv[:, 768:]).astype(BF16)
+        for t in range(2):
+            ts = pl.ds(t * rows, rows)
+            stats = jnp.zeros((rows, 128), F32)
+            for p in range(3):
+                ps = pl.ds(p * 128, 128)
+                q = qb[ts, ps]
+                wide = jnp.concatenate([values[:, p * 128:(p + 1) * 128], ones], axis=1)
+                for u in range(2):
+                    h = 2 * p + u
+                    scores = mm_nt(
+                        jnp.where((lanes >= 64) == (u == 1), q, jnp.zeros_like(q)), keys[:, p * 128:(p + 1) * 128]
+                    )
+                    top = jnp.max(scores, axis=-1, keepdims=True)
+                    if g > 0:
+                        before = tops[h, ts, :]
+                        top = jnp.maximum(before[:, :1], top)
+                    both = mm(jnp.exp(scores - top).astype(BF16), wide)
+                    if g > 0:
+                        fade = jnp.exp(before - top)
+                        both = both + jnp.concatenate([fade, fade], axis=1) * mixes[h, ts, :]
+                    if g < groups - 1:
+                        tops[h, ts, :] = jnp.broadcast_to(top, (rows, 128))
+                        mixes[h, ts, :] = both
+                        continue
+                    total = both[:, 128:]
+                    part = both[:, :128] / total
+                    mixed = part if u == 0 else jnp.where(lanes < 64, mixed, part)
+                    lse = top + jnp.log(total)
+                    s0 = lse.astype(BF16).astype(F32)
+                    s1 = (lse - s0).astype(BF16).astype(F32)
+                    s2 = lse - s0 - s1
+                    stats = jnp.where(
+                        lanes == h, s0, jnp.where(lanes == 8 + h, s1, jnp.where(lanes == 16 + h, s2, stats))
+                    )
+                if g == groups - 1:
+                    outb[pl.ds(t * 4, 4), :, ps] = mixed.astype(BF16).reshape(4, PAR, 128)
+            if g == groups - 1:
+                outb[pl.ds(t * 4, 4), :, 384:] = stats.astype(BF16).reshape(4, PAR, 128)
+                for o in range(4 * t, 4 * t + 4):
+                    @pl.when(sp != o)
+                    def _():
+                        push(outb.at[o], inb.at[sp], 3, (o, sc)).start()
+
     inb[sp] = outb[sp]
     push(outb.at[pl.ds(0, N_SPACE - 1)], inb.at[pl.ds(0, N_SPACE - 1)], 3, here).wait()
 
@@ -347,6 +373,7 @@
             pltpu.VMEM((4, 7, 4, 16, 384), BF16),
             pltpu.VMEM((256, 384), F32),
             pltpu.VMEM((2, 256, 384), BF16),
+            pltpu.VMEM((256, 1536), BF16),
             pltpu.VMEM((8, 4, 4, 16, 384), BF16),
             pltpu.VMEM((256, 384), F32),
             pltpu.VMEM((256, 128), F32),
@@ -363,14 +390,15 @@
             pltpu.VMEM((N_SPACE, PAR, 384), BF16),
             pltpu.VMEM((N_SCENE, PAR, 384), BF16),
             pltpu.VMEM((N_SPACE * PAR, 384), BF16),
-            pltpu.VMEM((N_SCENE * PAR, 384), BF16),
-            pltpu.VMEM((N_SCENE * PAR, 768), BF16),
+            pltpu.VMEM((6, N_SPACE * PAR, 128), F32),
+            pltpu.VMEM((6, N_SPACE * PAR, 256), F32),
             pltpu.VMEM((N_SPACE, PAR, 512), BF16),
             pltpu.VMEM((N_SPACE, PAR, 512), BF16),
             dma((7,)),
             dma((8,)),
-            dma((6,)),
-            dma((6,)),
+            dma((10,)),
+            dma((10,)),
+            pltpu.SemaphoreType.REGULAR,
         ],
         compiler_params=pltpu.CompilerParams(vmem_limit_bytes=63 << 20, collective_id=0, has_side_effects=True),
         name="fused",

time: 80.1 us -> 71.4 us (0.89)
  the two profiles are of different devices: /device:TPU:25 before, /device:TPU:1 now
where the time goes in v3:
time: 71.4 us; the launch traced here: 71.2 us
  Pallas kernels  66.6 us (93%)
  local copies, waits for them, and re-layouts  3.86 us (5%)
    pallas_call x1, Pallas kernels, local(): pl.pallas_call(fused_kernel, out_shape=(jax.ShapeDtypeStruct((2, 16, 4, 1...  66.6 us
    unnamed x7, local copies, waits for them, and re-layouts  3.86 us

profile of v3, /device:TPU:1, one launch (start us, length us, event | category | flops | bytes accessed | tf_op | source)
XLA Modules:
  0.0 71.2 jit_solution(1731253396572957346)
XLA Ops:
  0.6 66.6 %fused.1 = (bf16[2,16,4,16,384]{4,3,2,1,0:T(8,128)(2,1)}, bf16[64,384]{1,0:T(8,128)(2,1)}, f32[1,64]{1,0:T(1,128)}) custom-call(bf16[2,16,4,16,384]{4,3,2,1,0:T(8,128)(2,1)} %bitcast.7, bf16[384,1536]{1,0:T(8,128)(2,1)} %w1_hbm.1, bf16[1536,384]{1,0:T(8,128)(2,1)} %w2_hbm.1, bf16[384,1152]{1,0:T(8,128)(2,1)} %wqkv_hbm.1, bf16[384,384]{1,0:T(8,128)(2,1)} %wout_hbm.1, ...), custom_call_target="tpu_custom_call" | custom-call | tf_op jit(solution)/shard_map/fused/pallas_call | solution.py:361
  67.3 0.0 copy-start
  67.3 0.0 copy-start.1
  67.3 2.7 %copy.22 = bf16[2,16,64,384]{3,2,1,0:T(8,128)(2,1)} copy(bf16[2,16,64,384]{3,2,1,0:T(8,128)(2,1)} %bitcast.6) | data formatting | bytes 3145728
  70.0 0.0 copy-done
  70.0 0.6 copy.23
  70.6 0.0 copy-done.1
  70.6 0.5 copy.24
Async XLA Ops:
  67.3 2.7 %copy-start = (bf16[64,384]{1,0:T(8,128)(2,1)S(1)}, bf16[64,384]{1,0:T(8,128)(2,1)}, u32[]{:S(2)}) copy-start(bf16[64,384]{1,0:T(8,128)(2,1)} %get-tuple-element.13) | copy-start | bytes 147460
  67.3 3.4 %copy-start.1 = (f32[1,64]{1,0:T(1,128)S(1)}, f32[1,64]{1,0:T(1,128)}, u32[]{:S(2)}) copy-start(f32[1,64]{1,0:T(1,128)} %get-tuple-element.8) | copy-start | bytes 772

commit v4 on v3

--- a/solution.py
+++ b/solution.py
@@ -16,7 +16,7 @@
 BF16 = jnp.bfloat16
 MESH = pl.DeviceIdType.MESH
 FLAT = pl.DeviceIdType.LOGICAL
-GROUP = 8
+GROUPS = ((0, 12), (12, 16))
 HOPS = (
     (0, 0), (0, 1), (0, 3), (1, 0), (3, 0), (1, 1), (1, 3), (3, 1),
     (3, 3), (2, 0), (0, 2), (2, 1), (2, 3), (1, 2), (3, 2), (2, 2),
@@ -64,8 +64,8 @@
     loads = [pltpu.make_async_copy(pix_hbm.at[s], xs.at[s, pl.ds(3, 16)], lsem.at[s]) for s in range(2)]
     pairs = ((w1_hbm, w1), (w2_hbm, w2), (wqkv_hbm, wqkv), (wout_hbm, wout), (embed_hbm, embed))
     loads += [pltpu.make_async_copy(a, b, lsem.at[2 + n]) for n, (a, b) in enumerate(pairs)]
-    for cp in loads:
-        cp.start()
+    for n in (0, 2, 3, 1, 4, 5, 6):
+        loads[n].start()
 
     barrier = pltpu.get_barrier_semaphore()
 
@@ -100,61 +100,59 @@
     ssum[...] = jnp.zeros_like(ssum)
     scnt[...] = jnp.zeros_like(scnt)
 
-    def place(k):
-        inner = k < 4
-        s = lax.rem(k, 4) // 2
-        r0 = jnp.where(inner, 4 + 4 * lax.rem(k, 2), 12 * lax.rem(k, 2))
-        return s, r0
+    def place(k, half):
+        return lax.rem(k, 2), jnp.where(k < 2, 4 + 4 * half, 12 * half)
 
     def conv(k):
-        s, r0 = place(k)
         slot = lax.rem(k, 2)
 
         def piece(r, c):
+            s, r0 = place(k, r // 4)
             cs = pl.ds(c * 128, 128)
             acc = [None] * 7
             for a in range(7):
-                x = xs[s, r0 + r + a, :, :, cs]
+                x = xs[s, r0 + r % 4 + a, :, :, cs]
                 for b in range(7):
                     p = x * taps[a * 7 + b, :, cs][None]
                     acc[b] = p if acc[b] is None else acc[b] + p
             for b in range(7):
-                vs[r, b, :, :, cs] = acc[b]
+                vs[r % 4, b, :, :, cs] = acc[b]
 
         def row(r):
-            sp32[pl.ds(r * 64, 64), :] = mm(shm[...], vs[r].reshape(448, 384)) + bias_ref[...][None, :]
+            sp32[pl.ds(r * 64, 64), :] = mm(shm[...], vs[r % 4].reshape(448, 384)) + bias_ref[...][None, :]
 
         def norm():
             nb[slot] = (layer_norm(sp32[...]) * gain_ref[...][None, :]).astype(BF16)
 
         steps = []
-        for r in range(4):
+        for r in range(8):
             steps += [lambda r=r, c=c: piece(r, c) for c in range(3)]
             steps.append(lambda r=r: row(r))
         return steps + [norm]
 
     def mlp(k):
-        s, r0 = place(k)
-
         def part(h):
             hs = pl.ds(h * 512, 512)
             hid[:, hs] = gelu(mm(nb[lax.rem(k, 2)], w1[:, hs])).astype(BF16)
 
         def finish():
-            cen = xs[s, pl.ds(r0 + 3, 4)].reshape(256, 384)
-            f = (cen.astype(F32) + ls_ref[...][None, :] * mm(hid[...], w2[...])).astype(BF16)
-            fb[k] = f.reshape(4, 4, 16, 384)
-            save(k).start()
-            slots = jnp.concatenate([slot_ref[s, pl.ds(r0 + r, 1), :] for r in range(4)], axis=1)
-            m = onehot(iota((256, 256), 0) == slots)
-            ssum[...] += mm(m, f)
-            scnt[...] += mm(m, jnp.ones((256, 128), BF16))
+            tail = mm(hid[...], w2[...])
+            for half in range(2):
+                s, r0 = place(k, half)
+                cen = xs[s, pl.ds(r0 + 3, 4)].reshape(256, 384)
+                f = (cen.astype(F32) + ls_ref[...][None, :] * tail[half * 256:(half + 1) * 256]).astype(BF16)
+                fb[2 * k + half] = f.reshape(4, 4, 16, 384)
+                save(k, half).start()
+                slots = jnp.concatenate([slot_ref[s, pl.ds(r0 + r, 1), :] for r in range(4)], axis=1)
+                m = onehot(iota((256, 256), 0) == slots)
+                ssum[...] += mm(m, f)
+                scnt[...] += mm(m, jnp.ones((256, 128), BF16))
 
         return [lambda h=h: part(h) for h in range(3)] + [finish]
 
-    def save(k):
-        s, r0 = place(k)
-        return pltpu.make_async_copy(fb.at[k], feat_hbm.at[s, pl.ds(r0, 4)], fsem.at[k])
+    def save(k, half):
+        s, r0 = place(k, half)
+        return pltpu.make_async_copy(fb.at[2 * k + half], feat_hbm.at[s, pl.ds(r0, 4)], fsem.at[2 * k + half])
 
     def run(*lists):
         total = max(len(x) for x in lists)
@@ -166,13 +164,12 @@
                     done[n] += 1
 
     loads[0].wait()
-    loads[1].wait()
     run(conv(0))
-    loads[2].wait()
-    loads[3].wait()
+    for cp in loads[1:4]:
+        cp.wait()
 
     def stage(k, carry):
-        @pl.when(k == 1)
+        @pl.when(k == 0)
         def _():
             pl.semaphore_wait(barrier, N_SPACE + N_SCENE - 2)
             for m in range(1, N_SCENE):
@@ -186,7 +183,7 @@
             def _():
                 to_next.start()
 
-        @pl.when(k == 3)
+        @pl.when(k == 1)
         def _():
             @pl.when(jnp.logical_not(first))
             def _():
@@ -201,8 +198,8 @@
         run(mlp(k), conv(k + 1))
         return carry
 
-    lax.fori_loop(0, 7, stage, 0)
-    run(mlp(7))
+    lax.fori_loop(0, 3, stage, 0)
+    run(mlp(3))
 
     inter = inter_ref[...]
     hot = onehot(iota((64, 256), 0) == inter // 128)
@@ -269,22 +266,22 @@
         return carry
 
     lax.fori_loop(1, N_SPACE, send_q, 0)
-    groups = N_SCENE // GROUP
+    groups = len(GROUPS)
     for n in range(1, N_SCENE):
         dx, dy = HOPS[n]
         to = lax.rem(sc // 4 + dx, 4) * 4 + lax.rem(lax.rem(sc, 4) + dy, 4)
-        push(ain, ak.at[n], 6 + n // GROUP, (sp, to)).start()
+        push(ain, ak.at[n], 6 + sum(n >= end for _, end in GROUPS), (sp, to)).start()
     push(aq.at[pl.ds(0, N_SPACE - 1)], aq.at[pl.ds(0, N_SPACE - 1)], 1, here).wait()
     qb[...] = (mm(aq[...].reshape(N_SPACE * PAR, 384), wqkv[:, :384]) * 0.125).astype(BF16)
 
     rows = N_SPACE * PAR // 2
     lanes = iota((rows, 128), 1)
-    ones = jnp.ones((GROUP * PAR, 128), BF16)
-    for g in range(groups):
-        low = max(GROUP * g, 1)
-        got = pl.ds(low, GROUP * (g + 1) - low)
+    for g, (begin, end) in enumerate(GROUPS):
+        ones = jnp.ones(((end - begin) * PAR, 128), BF16)
+        low = max(begin, 1)
+        got = pl.ds(low, end - low)
         push(ak.at[got], ak.at[got], 6 + g, here).wait()
-        keys_in = ak[pl.ds(GROUP * g, GROUP)].reshape(GROUP * PAR, 384)
+        keys_in = ak[pl.ds(begin, end - begin)].reshape((end - begin) * PAR, 384)
         keys = mm(keys_in, wqkv[:, 384:768]).astype(BF16)
         values = mm(keys_in, wqkv[:, 768:]).astype(BF16)
         for t in range(2):
@@ -347,10 +344,11 @@
     loss_ref[...] = log_total - picked
 
     def drain(k, carry):
-        save(k).wait()
+        save(k, 0).wait()
+        save(k, 1).wait()
         return carry
 
-    lax.fori_loop(0, 8, drain, 0)
+    lax.fori_loop(0, 4, drain, 0)
 
 
 def local(pixels, dw_kernel, dw_bias, norm_gain, w_expand, w_reduce, layer_scale, pixel_slot, intersection,
@@ -371,9 +369,9 @@
             pltpu.VMEM((2, 22, 4, 16, 384), BF16),
             pltpu.VMEM((49, 16, 384), BF16),
             pltpu.VMEM((4, 7, 4, 16, 384), BF16),
-            pltpu.VMEM((256, 384), F32),
-            pltpu.VMEM((2, 256, 384), BF16),
-            pltpu.VMEM((256, 1536), BF16),
+            pltpu.VMEM((512, 384), F32),
+            pltpu.VMEM((2, 512, 384), BF16),
+            pltpu.VMEM((512, 1536), BF16),
             pltpu.VMEM((8, 4, 4, 16, 384), BF16),
             pltpu.VMEM((256, 384), F32),
             pltpu.VMEM((256, 128), F32),

time: 71.4 us -> 70.2 us (0.983)
  Pallas kernels: 66.6 us -> 65.5 us
    pallas_call x1, Pallas kernels: 66.6 us -> 65.5 us  [local(): pl.pallas_call(fused_kernel, out_shape=(jax.ShapeDtypeStruct((2, 16, 4, 1...]
where the time goes in v4:
time: 70.2 us; the launch traced here: 70 us
  Pallas kernels  65.5 us (93%)
  local copies, waits for them, and re-layouts  3.86 us (5%)
    pallas_call x1, Pallas kernels, local(): pl.pallas_call(fused_kernel, out_shape=(jax.ShapeDtypeStruct((2, 16, 4, 1...  65.5 us
    unnamed x7, local copies, waits for them, and re-layouts  3.86 us

profile of v4, /device:TPU:1, one launch (start us, length us, event | category | flops | bytes accessed | tf_op | source)
XLA Modules:
  0.0 70.0 jit_solution(13883085564987637134)
XLA Ops:
  0.6 65.5 %fused.1 = (bf16[2,16,4,16,384]{4,3,2,1,0:T(8,128)(2,1)}, bf16[64,384]{1,0:T(8,128)(2,1)}, f32[1,64]{1,0:T(1,128)}) custom-call(bf16[2,16,4,16,384]{4,3,2,1,0:T(8,128)(2,1)} %bitcast.7, bf16[384,1536]{1,0:T(8,128)(2,1)} %w1_hbm.1, bf16[1536,384]{1,0:T(8,128)(2,1)} %w2_hbm.1, bf16[384,1152]{1,0:T(8,128)(2,1)} %wqkv_hbm.1, bf16[384,384]{1,0:T(8,128)(2,1)} %wout_hbm.1, ...), custom_call_target="tpu_custom_call" | custom-call | tf_op jit(solution)/shard_map/fused/pallas_call | solution.py:359
  66.1 0.0 copy-start
  66.2 0.0 copy-start.1
  66.2 2.7 %copy.22 = bf16[2,16,64,384]{3,2,1,0:T(8,128)(2,1)} copy(bf16[2,16,64,384]{3,2,1,0:T(8,128)(2,1)} %bitcast.6) | data formatting | bytes 3145728
  68.9 0.0 copy-done
  68.9 0.6 copy.23
  69.5 0.0 copy-done.1
  69.5 0.5 copy.24
Async XLA Ops:
  66.1 2.7 %copy-start = (bf16[64,384]{1,0:T(8,128)(2,1)S(1)}, bf16[64,384]{1,0:T(8,128)(2,1)}, u32[]{:S(2)}) copy-start(bf16[64,384]{1,0:T(8,128)(2,1)} %get-tuple-element.13) | copy-start | bytes 147460
  66.2 3.4 %copy-start.1 = (f32[1,64]{1,0:T(1,128)S(1)}, f32[1,64]{1,0:T(1,128)}, u32[]{:S(2)}) copy-start(f32[1,64]{1,0:T(1,128)} %get-tuple-element.8) | copy-start | bytes 772
